TPU v7x, 32 devices: a whole 2x2x4 slice. The times are simulated.
32 devices in a mesh: dp: 4 (over y, x), expert: 8 (over z, core).
Axes of the slice: x: 2, y: 2, z: 4, core: 2. Of those that a mesh axis runs over, the one named last changes fastest.
Arguments:
- tokens: bfloat16 [1024, 3584], P('expert', 'dp'), may hold values from -6 to 6
- expert_ids: int32 [1024, 8], P('expert'), may hold values from 0 to 7, as said below
- replica_choice: int32 [1024, 8], P('expert'), may hold values from 0 to 1, as said below
- gate_weights: float32 [1024, 8], P('expert'), may hold values from 0.1 to 1
- placement: int32 [4, 2], replicated, may hold values from 0 to 7, as said below
- capacity: int32 [12], replicated, may hold values from 16 to 32, as said below
- w_gate: bfloat16 [8, 2, 3584, 1024], P('expert', None, 'dp'), as said below
- w_up: bfloat16 [8, 2, 3584, 1024], P('expert', None, 'dp'), as said below
- w_down: bfloat16 [8, 2, 1024, 3584], P('expert', None, None, 'dp'), as said below
Outputs:
- combined: bfloat16 [1024, 3584], P('expert', 'dp')
Inputs may be any that keep to these rules, and one draw needn't show every extreme that they name: `expert_ids`: each row names 8 different experts; in every aligned block of 128 rows some hot expert is named by at least 64 rows. `replica_choice`: 1 only where the slot's expert is hot; in every aligned block of 128 rows both replicas of some hot expert whose replicas have capacity 32 receive 32 or more slots. `placement`: column 0 holds 4 different expert numbers; column 1 holds 4 different expert-axis indices, none of them the own index of a hot expert. Entry e below 8 belongs to expert e's own replica, entry 8 + j to the copy of expert placement[j, 0]; both replicas of some hot expert have capacity 32. w_gate[placement[j, 1], 1] equals w_gate[placement[j, 0], 0]; entry [h, 1] is zero where index h hosts no copy. `w_up`: laid out as w_gate. `w_down`: laid out as w_gate.
All inputs are finite; a program needn't handle non-finite values.
Results may differ from a plain program's by a relative error of at most 0.0057.
Values may be sent and summed in bfloat16 or wider, within the bound.
No kernel may reach another device: no remote copies, remote signals or barrier semaphores. Data moves between devices by JAX's collectives and lax.ppermute only.
A program may use at most 128 MiB of HBM per device.

v0:
```python
import jax
import jax.numpy as jnp
from jax import lax
from jax.sharding import PartitionSpec as P


def slot_room(token_count, top_count, expert_count):
    return max(2, min(token_count // 4, 3 * token_count * top_count // (4 * expert_count)))


def on_device(
    tokens, expert_ids, replica_choice, gate_weights, placement, capacity, w_gate, w_up, w_down
):
    expert_count = lax.axis_size("expert")
    token_count, columns = tokens.shape
    top_count = expert_ids.shape[1]
    hot_count = placement.shape[0]
    replicas = expert_count + hot_count
    room_each = slot_room(token_count, top_count, expert_count)
    buffer_slots = expert_count * 2 * room_each
    slot_count = token_count * top_count
    hot_ids = placement[:, 0]
    flat_ids = expert_ids.reshape(-1)
    copy_flag = replica_choice.reshape(-1)
    hot_match = (flat_ids[:, None] == hot_ids[None, :]).astype(jnp.int32)
    hot_slot = jnp.sum(hot_match * jnp.arange(hot_count, dtype=jnp.int32)[None, :], 1)
    target = jnp.where(copy_flag == 1, expert_count + hot_slot, flat_ids)
    onehot = (target[:, None] == jnp.arange(replicas, dtype=jnp.int32)[None, :]).astype(jnp.int32)
    before = jnp.cumsum(onehot, 0) - onehot
    slot_rank = jnp.sum(before * onehot, 1)
    slot_limit = jnp.sum(onehot * capacity[None, :], 1)
    retained = slot_rank < slot_limit
    own_gate = w_gate[0, 0]
    own_up = w_up[0, 0]
    own_down = w_down[0, 0]
    position = jnp.where(retained, (flat_ids * 2 + copy_flag) * room_each + slot_rank, buffer_slots)
    source = jnp.full((buffer_slots,), slot_count, jnp.int32)
    source = source.at[position].set(jnp.arange(slot_count, dtype=jnp.int32), mode="drop")
    filled = source < slot_count
    token_rows = tokens[jnp.minimum(source, slot_count - 1) // top_count]
    outgoing = jnp.where(filled[:, None], token_rows, jnp.zeros((), tokens.dtype)).reshape(
        expert_count, 2, room_each, columns
    )
    received = lax.all_to_all(outgoing, "expert", split_axis=0, concat_axis=0, tiled=True)
    gate_part = jnp.einsum("nkcd,df->nkcf", received, own_gate, preferred_element_type=jnp.float32)
    up_part = jnp.einsum("nkcd,df->nkcf", received, own_up, preferred_element_type=jnp.float32)
    gate_part, up_part = (
        lax.psum_scatter(gate_part, "dp", scatter_dimension=3, tiled=True),
        lax.psum_scatter(up_part, "dp", scatter_dimension=3, tiled=True),
    )
    hidden = (jax.nn.silu(gate_part) * up_part).astype(jnp.bfloat16)
    hidden = lax.all_gather(hidden, "dp", axis=3, tiled=True)
    result = jnp.einsum("nkcf,fd->nkcd", hidden, own_down, preferred_element_type=jnp.float32)
    result = result.astype(jnp.bfloat16)
    returned = lax.all_to_all(result, "expert", split_axis=0, concat_axis=0, tiled=True)
    returned_flat = returned.reshape(buffer_slots, columns)
    picked = returned_flat[jnp.minimum(position, buffer_slots - 1)]
    weight = jnp.where(retained, gate_weights.reshape(-1), jnp.zeros((), jnp.float32))
    combined = jnp.sum(
        (weight[:, None] * picked.astype(jnp.float32)).reshape(token_count, top_count, columns), 1
    )
    return combined.astype(jnp.bfloat16)


def solution(mesh):
    return jax.shard_map(
        on_device,
        mesh=mesh,
        in_specs=(
            P("expert", "dp"),
            P("expert", None),
            P("expert", None),
            P("expert", None),
            P(),
            P(),
            P("expert", None, "dp", None),
            P("expert", None, "dp", None),
            P("expert", None, None, "dp"),
        ),
        out_specs=P("expert", "dp"),
        check_vma=False,
    )
```

profile of v0, /device:TPU:0, one launch (start us, length us, event | category | flops | bytes accessed | tf_op | source)
XLA Modules:
  0.0 200.4 jit_solution(12170056741895143210)
XLA Ops:
  6.5 0.8 copy.22
  7.4 0.1 eq.58
  7.5 0.1 reshape.159
  7.6 0.7 broadcast_compare_fusion
  8.2 0.1 copy.21
  8.4 0.1 eq.66
  8.5 0.1 eq.57
  8.6 0.7 add_multiply_fusion
  9.3 0.7 slice_bitcast_fusion
  10.1 3.4 %reduce-window.6 = s32[12,8,128]{2,1,0:T(8,128)S(1)} reduce-window(s32[12,8,128]{2,1,0:T(8,128)S(1)} %fusion.15, s32[]{:T(128)} %constant.14.clone.1), window={size=1x1x128 pad=0_0x0_0x127_0}, to_apply=%region_1.2 | reduce-window | flops 1560576 | bytes 98308 | tf_op jit(solution)/shard_map/reduce-window
  13.6 0.1 copy.25
  13.9 0.1 copy.28
  14.1 0.1 mul.83
  14.2 0.7 select_reduce_fusion
  14.9 4.3 %scatter_custom_fusion = s32[512]{0:T(512)S(1)} fusion(s32[1024]{0:T(1024)S(1)} %bitcast.57, s32[1024]{0:T(1024)S(1)} %iota.15, s32[]{:T(128)} %constant.15.clone.1), kind=kCustom, calls=%fused_computation.45 | custom fusion | bytes 2052 | tf_op jit(solution)/shard_map/scatter | solution.py:38
  19.3 0.1 broadcast_in_dim.35
  19.4 2.1 %gather_fusion = bf16[512,896]{1,0:T(8,128)(2,1)S(1)} fusion(bf16[128,896]{1,0:T(8,128)(2,1)S(1)} %copy-done, s32[1024]{0:T(1024)S(1)} %pad_clamp_fusion), kind=kCustom, calls=%fused_computation | custom fusion | bytes 1837056 | tf_op jit(solution)/shard_map/gather | solution.py:40
  21.5 0.2 broadcast_select_fusion
  21.6 30.2 %all_to_all.10 = bf16[8,2,32,896]{3,2,1,0:T(8,128)(2,1)S(1)} all-to-all(bf16[8,2,32,896]{3,2,1,0:T(8,128)(2,1)S(1)} %broadcast_select_fusion), channel_id=1, replica_groups=mesh['dp'=4,'expert'=8] {'expert'}, dimensions={0} | all-to-all | bytes 1835008 | tf_op jit(solution)/shard_map/all_to_all | solution.py:44
  51.8 2.6 %fusion.5 = f32[8,2,32,1024]{3,2,1,0:T(8,128)} fusion(bf16[8,2,32,896]{3,2,1,0:T(8,128)(2,1)S(1)} %all_to_all.10, bf16[1,2,896,1024]{3,2,1,0:T(8,128)(2,1)S(1)} %copy-done.2), kind=kOutput, calls=%fused_computation.9 | convolution fusion | flops 939524096 | bytes 4849664 | tf_op jit(solution)/shard_map/nkcd,df->nkcf/dot_general | solution.py:45
  54.5 4.1 %fusion.3 = f32[8,2,32,1024]{3,2,1,0:T(8,128)} fusion(bf16[8,2,32,896]{3,2,1,0:T(8,128)(2,1)S(1)} %all_to_all.10, bf16[1,2,896,1024]{3,2,1,0:T(8,128)(2,1)} %param.16), kind=kOutput, calls=%fused_computation.7 | convolution fusion | flops 939524096 | bytes 4849664 | tf_op jit(solution)/shard_map/nkcd,df->nkcf/dot_general | solution.py:46
  58.7 30.1 %reduce-scatter.3.cloned.1.call-done = f32[8,2,32,256]{3,2,1,0:T(8,128)} async-done(((f32[8,2,32,1024]{3,2,1,0:T(8,128)}), f32[8,2,32,256]{3,2,1,0:T(8,128)}) %reduce-scatter.3.cloned.1.call-update) | async-done | bytes 524304 | tf_op jit(solution)/shard_map/reduce_scatter | solution.py:48
  88.7 38.2 %reduce-scatter.5.cloned.1.call-done = f32[8,2,32,256]{3,2,1,0:T(8,128)} async-done(((f32[8,2,32,1024]{3,2,1,0:T(8,128)}), f32[8,2,32,256]{3,2,1,0:T(8,128)}) %reduce-scatter.5.cloned.1.call-update) | async-done | bytes 524304 | tf_op jit(solution)/shard_map/reduce_scatter | solution.py:49
  126.9 2.1 %multiply_convert_fusion = bf16[8,2,32,256]{3,2,1,0:T(8,128)(2,1)} fusion(f32[8,2,32,256]{3,2,1,0:T(8,128)} %reduce-scatter.5.cloned.1.call-done, f32[8,2,32,256]{3,2,1,0:T(8,128)} %reduce-scatter.3.cloned.1.call-done), kind=kLoop, calls=%fused_computation.16 | loop fusion | flops 786432 | bytes 1310720 | tf_op jit(solution)/shard_map/convert_element_type | solution.py:51
  129.0 26.5 %all-gather.2.cloned.1.call-done = bf16[8,2,32,1024]{3,2,1,0:T(8,128)(2,1)} async-done(((bf16[8,2,32,256]{3,2,1,0:T(8,128)(2,1)}), bf16[8,2,32,1024]{3,2,1,0:T(8,128)(2,1)}) %all-gather.2.cloned.1.call-update) | async-done | bytes 1048592 | tf_op jit(solution)/shard_map/all_gather | solution.py:52
  155.5 4.0 %fusion.10 = bf16[8,2,32,896]{3,2,1,0:T(8,128)(2,1)} fusion(bf16[8,2,32,1024]{3,2,1,0:T(8,128)(2,1)} %all-gather.2.cloned.1.call-done, bf16[1,2,1024,896]{3,2,1,0:T(8,128)(2,1)} %param.17), kind=kOutput, calls=%fused_computation.14 | convolution fusion | flops 939982848 | bytes 3801088 | tf_op jit(solution)/shard_map/nkcf,fd->nkcd/dot_general | solution.py:53
  159.6 4.6 %all-to-all-start.1 = ((bf16[8,2,32,896]{3,2,1,0:T(8,128)(2,1)}), bf16[8,2,32,896]{3,2,1,0:T(8,128)(2,1)S(1)}, u32[]{:S(2)}, u32[]{:S(2)}) async-start(bf16[8,2,32,896]{3,2,1,0:T(8,128)(2,1)} %fusion.10), calls=%async_computation.3 | async-start | bytes 1835008 | tf_op jit(solution)/shard_map/all_to_all | solution.py:55
  164.2 0.1 lt.50
  164.3 0.1 copy.27
  164.4 23.5 %all-to-all-done.1 = bf16[8,2,32,896]{3,2,1,0:T(8,128)(2,1)S(1)} async-done(((bf16[8,2,32,896]{3,2,1,0:T(8,128)(2,1)}), bf16[8,2,32,896]{3,2,1,0:T(8,128)(2,1)S(1)}, u32[]{:S(2)}, u32[]{:S(2)}) %all-to-all-start.1) | async-done | bytes 917536 | tf_op jit(solution)/shard_map/all_to_all | solution.py:55
  187.9 4.0 %gather_fusion.1 = bf16[1024,896]{1,0:T(8,128)(2,1)S(1)} fusion(bf16[512,896]{1,0:T(8,128)(2,1)S(1)} %bitcast.49, s32[1024]{0:T(1024)S(1)} %broadcast_clamp_fusion), kind=kCustom, calls=%fused_computation.1 | custom fusion | bytes 3674112 | tf_op jit(solution)/shard_map/gather | solution.py:57
  192.0 1.8 fusion
  (32 shorter events, 0.6 us)
Async XLA Ops:
  6.5 12.8 %copy-start = (bf16[128,896]{1,0:T(8,128)(2,1)S(1)}, bf16[128,896]{1,0:T(8,128)(2,1)}, u32[]{:S(2)}) copy-start(bf16[128,896]{1,0:T(8,128)(2,1)} %param.9) | copy-start | bytes 688132
  6.5 82.2 %reduce-scatter.3.cloned.1.call-start = ((), (), s32[]{:S(2)}) async-start(), calls=%async_computation.4 | async-start | bytes 2621440 | tf_op jit(solution)/shard_map/reduce_scatter | solution.py:48
  21.4 30.4 %copy-start.2 = (bf16[1,2,896,1024]{3,2,1,0:T(8,128)(2,1)S(1)}, bf16[1,2,896,1024]{3,2,1,0:T(8,128)(2,1)}, u32[]{:S(2)}) copy-start(bf16[1,2,896,1024]{3,2,1,0:T(8,128)(2,1)} %param.15) | copy-start | bytes 11010052
  54.5 72.5 %reduce-scatter.5.cloned.1.call-start = ((), (), s32[]{:S(2)}) async-start(), calls=%async_computation.5 | async-start | bytes 2621440 | tf_op jit(solution)/shard_map/reduce_scatter | solution.py:49
  58.6 96.9 %all-gather.2.cloned.1.call-start = ((), (), s32[]{:S(2)}) async-start(), calls=%async_computation.6 | async-start | bytes 1310720 | tf_op jit(solution)/shard_map/all_gather | solution.py:52
  129.0 35.3 %copy-start.1 = (f32[128,8]{0,1:T(8,128)S(1)}, f32[128,8]{0,1:T(8,128)}, u32[]{:S(2)}) copy-start(f32[128,8]{0,1:T(8,128)} %param.12) | copy-start | bytes 12292
  159.6 28.4 %all-to-all-start.1 = ((bf16[8,2,32,896]{3,2,1,0:T(8,128)(2,1)}), bf16[8,2,32,896]{3,2,1,0:T(8,128)(2,1)S(1)}, u32[]{:S(2)}, u32[]{:S(2)}) async-start(bf16[8,2,32,896]{3,2,1,0:T(8,128)(2,1)} %fusion.10), calls=%async_computation.3 | async-start | bytes 1835008 | tf_op jit(solution)/shard_map/all_to_all | solution.py:55
Sparse Core Ops, SparseCore 0:
  54.6 34.1 reduce-scatter.2
  91.7 35.1 reduce-scatter.4
  129.1 26.3 all-gather.1
where the time goes:
time: 201 us; the launch traced here: 200 us
  waiting for transfers between devices  118 us (59%)
  blocking collectives  30.2 us (15%)
  between operations  13.3 us (7%)
  local copies, waits for them, and re-layouts  13.2 us (7%)
  matrix products  10.7 us (5%)
  other arithmetic  9.9 us (5%)
  starting transfers between devices  4.69 us (2%)
    reduce_scatter x1, waiting for transfers between devices, on_device(): lax.psum_scatter(up_part, 'dp', scatter_dimension=3, tiled=True)  38.2 us
    all_to_all x1, blocking collectives, on_device(): lax.all_to_all(outgoing, 'expert', split_axis=0, concat_axis=0, tiled=True)  30.2 us
    reduce_scatter x1, waiting for transfers between devices, on_device(): lax.psum_scatter(gate_part, 'dp', scatter_dimension=3, tiled=True)  30.1 us
    all_gather x1, waiting for transfers between devices, on_device(): hidden = lax.all_gather(hidden, 'dp', axis=3, tiled=True)  26.5 us
    all_to_all x1, waiting for transfers between devices, on_device(): lax.all_to_all(result, 'expert', split_axis=0, concat_axis=0, tiled=True)  23.5 us
    all_to_all x1, starting transfers between devices, on_device(): lax.all_to_all(result, 'expert', split_axis=0, concat_axis=0, tiled=True)  4.61 us
    scatter x1, local copies, waits for them, and re-layouts, on_device(): source.at[position]  4.3 us
    dot_general x1, matrix products, on_device(): jnp.einsum('nkcd,df->nkcf', received, own_up, preferred_element_type=jnp....  4.08 us
  transfers between devices with their start and end apart: 4, of which 4 were waited for; matrix products, arithmetic and copies ran while one was open for 2% of the time, Pallas kernels for 0%

commit v1 on v0

v1 whole, which is shorter than its diff:
```python
import functools

import jax
import jax.numpy as jnp
from jax import lax
from jax.experimental import pallas as pl
from jax.experimental.pallas import tpu as pltpu
from jax.sharding import PartitionSpec as P

BF16 = jnp.bfloat16
F32 = jnp.float32
I32 = jnp.int32
DIRECT_LIMIT = 8


def round_up(n, m):
    return -(-n // m) * m


def slot_room(token_count, top_count, expert_count):
    return max(2, min(token_count // 4, 3 * token_count * top_count // (4 * expert_count)))


def dot(a, b):
    return jnp.dot(a, b, preferred_element_type=F32)


def vmem_specs(n):
    return [pl.BlockSpec(memory_space=pltpu.VMEM)] * n


SMEM_SPEC = pl.BlockSpec(memory_space=pltpu.SMEM)


def route_kernel(
    sizes, flip, place, cap, ids_ref, choice_ref, gate_ref, tok_ref, high_ref, low_ref, *out_refs
):
    experts, hot, room, half, room_a, room_b = sizes
    count, top = ids_ref.shape
    per = room_a + room_b
    columns = experts * per
    ids, choice, gate = ids_ref[...], choice_ref[...], gate_ref[...]
    lane = lax.broadcasted_iota(I32, (count, 2 * experts), 1)
    key = ids + experts * choice
    member = jnp.zeros((count, 2 * experts), F32)
    weight = jnp.zeros((count, 2 * experts), F32)
    for k in range(top):
        hit = key[:, k : k + 1] == lane
        member = jnp.where(hit, 1.0, member)
        weight = jnp.where(hit, gate[:, k : k + 1], weight)
    earlier = lax.broadcasted_iota(I32, (count, count), 1) < lax.broadcasted_iota(
        I32, (count, count), 0
    )
    rank = dot(jnp.where(earlier, 1.0, 0.0).astype(BF16), member.astype(BF16))
    lane_row = lax.broadcasted_iota(I32, (1, 2 * experts), 1)
    limit = jnp.zeros((1, 2 * experts), I32)
    for e in range(experts):
        limit = jnp.where(lane_row == e, cap[e], limit)
    for j in range(hot):
        limit = jnp.where(lane_row == place[j, 0] + experts, cap[experts + j], limit)
    kept = (member > 0.5) & (rank < limit.astype(F32))
    rank = jnp.where(kept, rank, -1.0)

    column = lax.broadcasted_iota(I32, (1, columns), 1)
    block = jnp.floor((column.astype(F32) + 0.5) * (1.0 / per)).astype(I32)
    slot = column - block * per
    dest = block ^ flip[0]
    pair_key = jnp.full((1, columns), -1, I32)
    start = jnp.zeros((1, columns), I32)
    for j in range(hot):
        owner, host = dest == place[j, 0], dest == place[j, 1]
        pair_key = jnp.where(owner | host, place[j, 0] + experts, pair_key)
        start = jnp.where(host, half, start)
    first = slot < room_a
    in_pair = slot - room_a
    wanted = jnp.where(first, dest, jnp.where(in_pair < half, pair_key, -1))
    place_rank = jnp.where(first, slot, in_pair + start).astype(F32)
    spread = jnp.where(
        lax.broadcasted_iota(I32, (2 * experts, columns), 0) == wanted, 1.0, 0.0
    ).astype(BF16)
    usable = jnp.max(spread.astype(F32), axis=0, keepdims=True) > 0.5
    chosen = (dot(rank.astype(BF16), spread) == place_rank) & usable
    weight_high = weight.astype(BF16)
    weight_low = (weight - weight_high.astype(F32)).astype(BF16)
    high_ref[...] = jnp.where(chosen, dot(weight_high, spread), 0.0).astype(BF16)
    low_ref[...] = jnp.where(chosen, dot(weight_low, spread), 0.0).astype(BF16)
    picks = jnp.where(chosen, 1.0, 0.0).T.astype(BF16)
    rows = dot(picks, tok_ref[...]).astype(BF16)
    for i, ref in enumerate(out_refs):
        ref[...] = rows[i * per : (i + 1) * per]


def up_kernel(sizes, at, *refs):
    experts, parts, room_a, room_b = sizes
    x_refs = refs[:experts]
    wg0, wg1, wu0, wu1 = refs[experts : experts + 4]
    outs = refs[experts + 4 : experts + 4 + parts]
    xa, xb, acc_a, acc_b = refs[experts + 4 + parts :]

    @pl.when(pl.program_id(0) == 0)
    def _():
        for i, ref in enumerate(x_refs):
            xa[i * room_a : (i + 1) * room_a] = ref[:room_a]
            xb[i * room_b : (i + 1) * room_b] = ref[room_a:]

    rows_a, rows_b = experts * room_a // parts, experts * room_b // parts
    for g, (first, second) in enumerate(((wg0, wg1), (wu0, wu1))):
        acc_a[...] = dot(xa[...], first[0, 0])
        acc_b[...] = dot(xb[...], second[0, 0])
        for k, out in enumerate(outs):
            q = at[0] ^ k
            out[g, :rows_a] = acc_a[pl.ds(q * rows_a, rows_a)].astype(out.dtype)
            out[g, rows_a:] = acc_b[pl.ds(q * rows_b, rows_b)].astype(out.dtype)


def hidden_kernel(own, *refs):
    out = refs[-1]
    total = own[...]
    for ref in refs[:-1]:
        total += ref[...].astype(F32)
    out[...] = (jax.nn.silu(total[0]) * total[1]).astype(BF16)


def down_kernel(sizes, at, *refs):
    experts, parts, room_a, room_b = sizes
    hids = refs[:parts]
    w0, w1 = refs[parts : parts + 2]
    outs = refs[parts + 2 : parts + 2 + experts]
    ha, hb = refs[parts + 2 + experts :]
    rows_a, rows_b = experts * room_a // parts, experts * room_b // parts
    for k, ref in enumerate(hids):
        q = at[0] ^ k
        ha[pl.ds(q * rows_a, rows_a)] = ref[:rows_a]
        hb[pl.ds(q * rows_b, rows_b)] = ref[rows_a:]
    ra = dot(ha[...], w0[0, 0]).astype(BF16)
    rb = dot(hb[...], w1[0, 0]).astype(BF16)
    for i, out in enumerate(outs):
        out[:room_a] = ra[i * room_a : (i + 1) * room_a]
        out[room_a:] = rb[i * room_b : (i + 1) * room_b]


def combine_kernel(high, low, *refs):
    out, res = refs[-2:]
    per = refs[0].shape[0]
    for i, ref in enumerate(refs[:-2]):
        res[i * per : (i + 1) * per] = ref[...]
    rows = res[...]
    out[...] = (dot(high[...], rows) + dot(low[...], rows)).astype(BF16)


def flips(n, j):
    return [(i, i ^ j) for i in range(n)]


def exchange(pieces, axis):
    n = len(pieces)
    if n <= DIRECT_LIMIT:
        return [pieces[0]] + [lax.ppermute(x, axis, flips(n, j)) for j, x in enumerate(pieces) if j]
    moved = lax.all_to_all(jnp.stack(pieces), axis, split_axis=0, concat_axis=0, tiled=True)
    return [moved[i] for i in range(n)]


def on_device(
    tokens, expert_ids, replica_choice, gate_weights, placement, capacity, w_gate, w_up, w_down
):
    experts = lax.axis_size("expert")
    parts = lax.axis_size("dp")
    me = lax.axis_index("expert")
    count, cols = tokens.shape
    ff = w_gate.shape[3]
    hot = placement.shape[0]
    room = slot_room(count, expert_ids.shape[1], experts)
    half = -(-room // 2)
    room_a, room_b = round_up(room, 16), round_up(half, 16)
    per = room_a + room_b
    direct = experts <= DIRECT_LIMIT
    flip = jnp.where(direct, me, 0).astype(I32).reshape(1)
    hosting = jnp.any(placement[:, 1] == me)
    second = hosting.astype(I32)
    at = lax.axis_index("dp").astype(I32).reshape(1)

    sds = jax.ShapeDtypeStruct
    high, low, *pieces = pl.pallas_call(
        functools.partial(route_kernel, (experts, hot, room, half, room_a, room_b)),
        out_shape=[sds((count, experts * per), BF16)] * 2 + [sds((per, cols), BF16)] * experts,
        in_specs=[SMEM_SPEC] * 3 + vmem_specs(4),
        out_specs=vmem_specs(2 + experts),
        name="route",
    )(flip, placement, capacity, expert_ids, replica_choice, gate_weights, tokens)
    arrived = exchange(pieces, "expert")

    block = 256 if ff % 256 == 0 else ff
    rows = experts * per // parts
    scalars = jnp.concatenate([at, second.reshape(1)])
    w_specs = [
        pl.BlockSpec((1, 1, cols, block), lambda f, s: (0, 0, 0, f)),
        pl.BlockSpec((1, 1, cols, block), lambda f, s: (0, s[1], 0, f)),
    ]
    sums = pl.pallas_call(
        functools.partial(up_kernel, (experts, parts, room_a, room_b)),
        out_shape=[sds((2, rows, ff), F32)] + [sds((2, rows, ff), BF16)] * (parts - 1),
        grid_spec=pltpu.PrefetchScalarGridSpec(
            num_scalar_prefetch=1,
            grid=(ff // block,),
            in_specs=[pl.BlockSpec((per, cols), lambda f, s: (0, 0))] * experts + w_specs * 2,
            out_specs=[pl.BlockSpec((2, rows, block), lambda f, s: (0, 0, f))] * parts,
            scratch_shapes=[
                pltpu.VMEM((experts * room_a, cols), BF16),
                pltpu.VMEM((experts * room_b, cols), BF16),
                pltpu.VMEM((experts * room_a, block), F32),
                pltpu.VMEM((experts * room_b, block), F32),
            ],
        ),
        name="gate_up",
    )(scalars, *arrived, w_gate, w_gate, w_up, w_up)
    sums = [sums[0]] + [lax.ppermute(x, "dp", flips(parts, j)) for j, x in enumerate(sums) if j]
    hidden = pl.pallas_call(
        hidden_kernel,
        out_shape=sds((rows, ff), BF16),
        in_specs=vmem_specs(parts),
        out_specs=vmem_specs(1)[0],
        name="hidden",
    )(*sums)
    spread = [hidden] + [lax.ppermute(hidden, "dp", flips(parts, j)) for j in range(1, parts)]
    results = pl.pallas_call(
        functools.partial(down_kernel, (experts, parts, room_a, room_b)),
        out_shape=[sds((per, cols), BF16)] * experts,
        grid_spec=pltpu.PrefetchScalarGridSpec(
            num_scalar_prefetch=1,
            grid=(1,),
            in_specs=[pl.BlockSpec((rows, ff), lambda f, s: (0, 0))] * parts
            + [
                pl.BlockSpec((1, 1, ff, cols), lambda f, s: (0, 0, 0, 0)),
                pl.BlockSpec((1, 1, ff, cols), lambda f, s: (0, s[1], 0, 0)),
            ],
            out_specs=[pl.BlockSpec((per, cols), lambda f, s: (0, 0))] * experts,
            scratch_shapes=[
                pltpu.VMEM((experts * room_a, ff), BF16),
                pltpu.VMEM((experts * room_b, ff), BF16),
            ],
        ),
        name="down",
    )(scalars, *spread, w_down, w_down)
    returned = exchange(results, "expert")
    return pl.pallas_call(
        combine_kernel,
        out_shape=sds((count, cols), BF16),
        in_specs=vmem_specs(2 + experts),
        out_specs=vmem_specs(1)[0],
        scratch_shapes=[pltpu.VMEM((experts * per, cols), BF16)],
        name="combine",
    )(high, low, *returned)


def solution(mesh):
    return jax.shard_map(
        on_device,
        mesh=mesh,
        in_specs=(
            P("expert", "dp"),
            P("expert", None),
            P("expert", None),
            P("expert", None),
            P(),
            P(),
            P("expert", None, "dp", None),
            P("expert", None, "dp", None),
            P("expert", None, None, "dp"),
        ),
        out_specs=P("expert", "dp"),
        check_vma=False,
    )
```

time: 201 us -> 103 us (0.51)
  waiting for transfers between devices: 118 us -> 42 us
  blocking collectives: 30.2 us -> 0 us
  starting transfers between devices: 4.69 us -> 27.3 us
  Pallas kernels: 0 us -> 19.5 us
  between operations: 13.3 us -> 0.8 us
  matrix products: 10.7 us -> 0 us
  other arithmetic: 9.9 us -> 1.95 us
  local copies, waits for them, and re-layouts: 13.2 us -> 9.02 us
    reduce_scatter x2 -> x0, waiting for transfers between devices: 68.2 us -> none  [the longest x1 38.2 us: on_device(): lax.psum_scatter(up_part, 'dp', scatter_dimension=3, tiled=True)]
    ppermute x0 -> x20, waiting for transfers between devices: none -> 42 us  [the longest x3 17.6 us: on_device(): lax.ppermute(x, 'dp', flips(parts, j))]
    all_to_all x1 -> x0, blocking collectives: 30.2 us -> none  [on_device(): lax.all_to_all(outgoing, 'expert', split_axis=0, concat_axis=0, tiled=True)]
    ppermute x0 -> x20, starting transfers between devices: none -> 27.3 us  [the longest x14 20.3 us: exchange(): lax.ppermute(x, axis, flips(n, j))]
    all_gather x1 -> x0, waiting for transfers between devices: 26.5 us -> none  [on_device(): hidden = lax.all_gather(hidden, 'dp', axis=3, tiled=True)]
    all_to_all x1 -> x0, waiting for transfers between devices: 23.5 us -> none  [on_device(): lax.all_to_all(result, 'expert', split_axis=0, concat_axis=0, tiled=True)]
    pallas_call x0 -> x5, Pallas kernels: none -> 19.5 us  [the longest x1 7.12 us: on_device(): pl.pallas_call(functools.partial(up_kernel, (experts, parts, room_a, room...]
    dot_general x3 -> x0, matrix products: 10.7 us -> none  [the longest x1 4.08 us: on_device(): jnp.einsum('nkcd,df->nkcf', received, own_up, preferred_element_type=jnp....]
  transfers between devices with their start and end apart: 4 -> 20, of which waited for: 4 -> 9; matrix products, arithmetic and copies ran while one was open for 2% -> 2% of each run, Pallas kernels for 0% -> 0%
where the time goes in v1:
time: 103 us; the launch traced here: 101 us
  waiting for transfers between devices  42 us (41%)
  starting transfers between devices  27.3 us (27%)
  Pallas kernels  19.5 us (19%)
  local copies, waits for them, and re-layouts  9.02 us (9%)
  other arithmetic  1.95 us (2%)
    ppermute x14, starting transfers between devices, exchange(): lax.ppermute(x, axis, flips(n, j))  20.3 us
    ppermute x3, waiting for transfers between devices, on_device(): lax.ppermute(x, 'dp', flips(parts, j))  17.6 us
    ppermute x14, waiting for transfers between devices, exchange(): lax.ppermute(x, axis, flips(n, j))  16.6 us
    unnamed x44, local copies, waits for them, and re-layouts  9.02 us
    ppermute x3, waiting for transfers between devices, on_device(): lax.ppermute(hidden, 'dp', flips(parts, j))  7.83 us
    pallas_call x1, Pallas kernels, on_device(): pl.pallas_call(functools.partial(up_kernel, (experts, parts, room_a, room...  7.12 us
    pallas_call x1, Pallas kernels, on_device(): pl.pallas_call(functools.partial(down_kernel, (experts, parts, room_a, ro...  4.94 us
    ppermute x3, starting transfers between devices, on_device(): lax.ppermute(x, 'dp', flips(parts, j))  3.55 us
  transfers between devices with their start and end apart: 20, of which 9 were waited for; matrix products, arithmetic and copies ran while one was open for 2% of the time, Pallas kernels for 0%

profile of v1, /device:TPU:0, one launch (start us, length us, event | category | flops | bytes accessed | tf_op | source)
XLA Modules:
  0.0 100.6 jit_solution(9741822910002801528)
XLA Ops:
  0.0 1.4 %copy.10.place = s32[4,2]{1,0:T(4,128)} copy(s32[4,2]{0,1:T(2,128)} %param.13) | data formatting | bytes 64 | tf_op args[4]
  1.4 1.4 %copy.11.ids_ref = s32[128,8]{1,0:T(8,128)} copy(s32[128,8]{0,1:T(8,128)} %param.10) | data formatting | bytes 8192 | tf_op args[1]
  2.8 1.4 %copy.12.choice_ref = s32[128,8]{1,0:T(8,128)} copy(s32[128,8]{0,1:T(8,128)} %param.11) | data formatting | bytes 8192 | tf_op args[2]
  4.2 1.4 %copy.13.gate_ref = f32[128,8]{1,0:T(8,128)} copy(f32[128,8]{0,1:T(8,128)} %param.12) | data formatting | bytes 8192 | tf_op args[3]
  5.6 2.8 %route.1 = (bf16[128,384]{1,0:T(8,128)(2,1)}, bf16[128,384]{1,0:T(8,128)(2,1)}, bf16[48,896]{1,0:T(8,128)(2,1)}, bf16[48,896]{1,0:T(8,128)(2,1)}, bf16[48,896]{1...) custom-call(s32[1]{0:T(128)} %bitcast.flip, ...), custom_call_target="tpu_custom_call" | custom-call | tf_op jit(solution)/shard_map/route/pallas_call | solution.py:183
  8.8 2.6 %collective-permute-start.1 = (bf16[48,896]{1,0:T(8,128)(2,1)}, bf16[48,896]{1,0:T(8,128)(2,1)S(1)}, u32[]{:S(2)}, u32[]{:S(2)}) collective-permute-start(bf16[48,896]{1,0:T(8,128)(2,1)} %get-tuple-element.31), channel_id=1, source_target_pairs={{0,2},{1,3},{2,0},{3,1},{4,6},{5,7},{6,4},{7,5},{8,10},{9,11},{10,... | collective-permute-start | bytes 258056 | tf_op jit(solution)/shard_map/ppermute | solution.py:158
  11.5 2.8 %collective-permute-start.3 = (bf16[48,896]{1,0:T(8,128)(2,1)}, bf16[48,896]{1,0:T(8,128)(2,1)S(1)}, u32[]{:S(2)}, u32[]{:S(2)}) collective-permute-start(bf16[48,896]{1,0:T(8,128)(2,1)} %get-tuple-element.33), channel_id=1, source_target_pairs={{0,4},{1,5},{2,6},{3,7},{4,0},{5,1},{6,2},{7,3},{8,12},{9,13},{10,... | collective-permute-start | bytes 258056 | tf_op jit(solution)/shard_map/ppermute | solution.py:158
  14.3 1.3 %compare_reduce_fusion = pred[]{:T(512)} fusion(s32[4,2]{0,1:T(2,128)} %param.13, s32[]{:T(128)} %axis_index.22), kind=kLoop, calls=%fused_computation | loop fusion | flops 7 | bytes 21 | tf_op jit(solution)/shard_map/reduce_or | solution.py:178
  16.3 3.7 %collective-permute-start.5 = (bf16[48,896]{1,0:T(8,128)(2,1)}, bf16[48,896]{1,0:T(8,128)(2,1)S(1)}, u32[]{:S(2)}, u32[]{:S(2)}) collective-permute-start(bf16[48,896]{1,0:T(8,128)(2,1)} %get-tuple-element.35), channel_id=1, source_target_pairs={{0,6},{1,7},{2,4},{3,5},{4,2},{5,3},{6,0},{7,1},{8,14},{9,15},{10,... | collective-permute-start | bytes 258056 | tf_op jit(solution)/shard_map/ppermute | solution.py:158
  20.1 0.6 pad_add_fusion.at
  20.7 6.7 %collective-permute-done.4.refs_5_ = bf16[48,896]{1,0:T(8,128)(2,1)S(1)} collective-permute-done((bf16[48,896]{1,0:T(8,128)(2,1)}, bf16[48,896]{1,0:T(8,128)(2,1)S(1)}, u32[]{:S(2)}, u32[]{:S(2)}) %collective-permute-start.4) | collective-permute-done | bytes 86048 | tf_op jit(solution)/shard_map/ppermute | solution.py:158
  28.1 7.1 %gate_up.1 = (f32[2,96,1024]{2,1,0:T(8,128)}, bf16[2,96,1024]{2,1,0:T(8,128)(2,1)}, bf16[2,96,1024]{2,1,0:T(8,128)(2,1)}, bf16[2,96,1024]{2,1,0:T(8,128)(2,1)}) custom-call(s32[2]{0:T(128)} %pad_add_fusion.at, bf16[48,896]{1,0:T(8,128)(2,1)} %get-tuple-element.29.refs_0_, bf16[48,896]{1,0:T(8,128)(2,1)} %copy-done.6, bf16[48,896]{1,0:T(8,128)(2,1)} %copy-done.7, ...), custom_call_target="tpu_custom_call" | custom-call | tf_op jit(solution)/shard_map/gate_up/pallas_call | solution.py:199
  35.2 1.6 %collective-permute-start.7 = (bf16[2,96,1024]{2,1,0:T(8,128)(2,1)}, bf16[2,96,1024]{2,1,0:T(8,128)(2,1)S(1)}, u32[]{:S(2)}, u32[]{:S(2)}) collective-permute-start(bf16[2,96,1024]{2,1,0:T(8,128)(2,1)} %get-tuple-element.38), channel_id=1, source_target_pairs={{0,8},{8,0},{16,24},{24,16},{1,9},{9,1},{17,25},{25,17},{2,10},{10... | collective-permute-start | bytes 1179656 | tf_op jit(solution)/shard_map/ppermute | solution.py:216
  36.8 1.5 %collective-permute-start.8 = (bf16[2,96,1024]{2,1,0:T(8,128)(2,1)}, bf16[2,96,1024]{2,1,0:T(8,128)(2,1)S(1)}, u32[]{:S(2)}, u32[]{:S(2)}) collective-permute-start(bf16[2,96,1024]{2,1,0:T(8,128)(2,1)} %get-tuple-element.39), channel_id=1, source_target_pairs={{0,16},{8,24},{16,0},{24,8},{1,17},{9,25},{17,1},{25,9},{2,18},{10... | collective-permute-start | bytes 1179656 | tf_op jit(solution)/shard_map/ppermute | solution.py:216
  38.8 8.7 %collective-permute-done.7.refs_0_ = bf16[2,96,1024]{2,1,0:T(8,128)(2,1)S(1)} collective-permute-done((bf16[2,96,1024]{2,1,0:T(8,128)(2,1)}, bf16[2,96,1024]{2,1,0:T(8,128)(2,1)S(1)}, u32[]{:S(2)}, u32[]{:S(2)}) %collective-permute-start.7) | collective-permute-done | bytes 393248 | tf_op jit(solution)/shard_map/ppermute | solution.py:216
  47.5 8.9 %collective-permute-done.8.refs_1_ = bf16[2,96,1024]{2,1,0:T(8,128)(2,1)S(1)} collective-permute-done((bf16[2,96,1024]{2,1,0:T(8,128)(2,1)}, bf16[2,96,1024]{2,1,0:T(8,128)(2,1)S(1)}, u32[]{:S(2)}, u32[]{:S(2)}) %collective-permute-start.8) | collective-permute-done | bytes 393248 | tf_op jit(solution)/shard_map/ppermute | solution.py:216
  56.4 0.7 copy-done.1
  57.3 2.4 %hidden.1.refs_0_ = bf16[96,1024]{1,0:T(8,128)(2,1)} custom-call(f32[2,96,1024]{2,1,0:T(8,128)} %get-tuple-element.37.own, bf16[2,96,1024]{2,1,0:T(8,128)(2,1)} %copy-done, bf16[2,96,1024]{2,1,0:T(8,128)(2,1)} %copy-done.1, bf16[2,96,1024]{2,1,0:T(8,128)(2,1)} %copy-done.2), custom_call_target="tpu_custom_call" | custom-call | tf_op jit(solution)/shard_map/hidden/pallas_call | solution.py:217
  59.7 1.5 %collective-permute-start.12 = (bf16[96,1024]{1,0:T(8,128)(2,1)}, bf16[96,1024]{1,0:T(8,128)(2,1)S(1)}, u32[]{:S(2)}, u32[]{:S(2)}) collective-permute-start(bf16[96,1024]{1,0:T(8,128)(2,1)} %hidden.1.refs_0_), channel_id=1, source_target_pairs={{0,24},{8,16},{16,8},{24,0},{1,25},{9,17},{17,9},{25,1},{2,26},{10... | collective-permute-start | bytes 589832 | tf_op jit(solution)/shard_map/ppermute | solution.py:224
  61.2 1.0 %collective-permute-start.11 = (bf16[96,1024]{1,0:T(8,128)(2,1)}, bf16[96,1024]{1,0:T(8,128)(2,1)S(1)}, u32[]{:S(2)}, u32[]{:S(2)}) collective-permute-start(bf16[96,1024]{1,0:T(8,128)(2,1)} %hidden.1.refs_0_), channel_id=1, source_target_pairs={{0,16},{8,24},{16,0},{24,8},{1,17},{9,25},{17,1},{25,9},{2,18},{10... | collective-permute-start | bytes 589832 | tf_op jit(solution)/shard_map/ppermute | solution.py:224
  62.2 0.9 collective-permute-start.10
  63.2 5.4 %collective-permute-done.12.refs_3_ = bf16[96,1024]{1,0:T(8,128)(2,1)S(1)} collective-permute-done((bf16[96,1024]{1,0:T(8,128)(2,1)}, bf16[96,1024]{1,0:T(8,128)(2,1)S(1)}, u32[]{:S(2)}, u32[]{:S(2)}) %collective-permute-start.12) | collective-permute-done | bytes 196640 | tf_op jit(solution)/shard_map/ppermute | solution.py:224
  68.6 2.2 %collective-permute-done.11.refs_2_ = bf16[96,1024]{1,0:T(8,128)(2,1)S(1)} collective-permute-done((bf16[96,1024]{1,0:T(8,128)(2,1)}, bf16[96,1024]{1,0:T(8,128)(2,1)S(1)}, u32[]{:S(2)}, u32[]{:S(2)}) %collective-permute-start.11) | collective-permute-done | bytes 196640 | tf_op jit(solution)/shard_map/ppermute | solution.py:224
  71.5 0.7 copy-done.5
  72.2 4.9 %down.1 = (bf16[48,896]{1,0:T(8,128)(2,1)}, bf16[48,896]{1,0:T(8,128)(2,1)}, bf16[48,896]{1,0:T(8,128)(2,1)}, bf16[48,896]{1,0:T(8,128)(2,1)}, bf16[48,896]{1,0:...) custom-call(s32[2]{0:T(128)} %pad_add_fusion.at, ...), custom_call_target="tpu_custom_call" | custom-call | tf_op jit(solution)/shard_map/down/pallas_call | solution.py:225
  77.1 4.0 %collective-permute-start.14 = (bf16[48,896]{1,0:T(8,128)(2,1)}, bf16[48,896]{1,0:T(8,128)(2,1)S(1)}, u32[]{:S(2)}, u32[]{:S(2)}) collective-permute-start(bf16[48,896]{1,0:T(8,128)(2,1)} %get-tuple-element.43), channel_id=1, source_target_pairs={{0,2},{1,3},{2,0},{3,1},{4,6},{5,7},{6,4},{7,5},{8,10},{9,11},{10,... | collective-permute-start | bytes 258056 | tf_op jit(solution)/shard_map/ppermute | solution.py:158
  81.2 3.2 %collective-permute-start.16 = (bf16[48,896]{1,0:T(8,128)(2,1)}, bf16[48,896]{1,0:T(8,128)(2,1)S(1)}, u32[]{:S(2)}, u32[]{:S(2)}) collective-permute-start(bf16[48,896]{1,0:T(8,128)(2,1)} %get-tuple-element.45), channel_id=1, source_target_pairs={{0,4},{1,5},{2,6},{3,7},{4,0},{5,1},{6,2},{7,3},{8,12},{9,13},{10,... | collective-permute-start | bytes 258056 | tf_op jit(solution)/shard_map/ppermute | solution.py:158
  84.4 2.1 %collective-permute-start.18 = (bf16[48,896]{1,0:T(8,128)(2,1)}, bf16[48,896]{1,0:T(8,128)(2,1)S(1)}, u32[]{:S(2)}, u32[]{:S(2)}) collective-permute-start(bf16[48,896]{1,0:T(8,128)(2,1)} %get-tuple-element.47), channel_id=1, source_target_pairs={{0,6},{1,7},{2,4},{3,5},{4,2},{5,3},{6,0},{7,1},{8,14},{9,15},{10,... | collective-permute-start | bytes 258056 | tf_op jit(solution)/shard_map/ppermute | solution.py:158
  86.5 1.2 %collective-permute-start.19 = (bf16[48,896]{1,0:T(8,128)(2,1)}, bf16[48,896]{1,0:T(8,128)(2,1)S(1)}, u32[]{:S(2)}, u32[]{:S(2)}) collective-permute-start(bf16[48,896]{1,0:T(8,128)(2,1)} %get-tuple-element.48), channel_id=1, source_target_pairs={{0,7},{1,6},{2,5},{3,4},{4,3},{5,2},{6,1},{7,0},{8,15},{9,14},{10,... | collective-permute-start | bytes 258056 | tf_op jit(solution)/shard_map/ppermute | solution.py:158
  88.1 9.5 %collective-permute-done.17.refs_5_ = bf16[48,896]{1,0:T(8,128)(2,1)S(1)} collective-permute-done((bf16[48,896]{1,0:T(8,128)(2,1)}, bf16[48,896]{1,0:T(8,128)(2,1)S(1)}, u32[]{:S(2)}, u32[]{:S(2)}) %collective-permute-start.17) | collective-permute-done | bytes 86048 | tf_op jit(solution)/shard_map/ppermute | solution.py:158
  97.6 0.6 copy-done.17
  98.3 2.4 %combine.1 = bf16[128,896]{1,0:T(8,128)(2,1)} custom-call(bf16[128,384]{1,0:T(8,128)(2,1)} %get-tuple-element.27.high, bf16[128,384]{1,0:T(8,128)(2,1)} %get-tuple-element.28.low, bf16[48,896]{1,0:T(8,128)(2,1)} %get-tuple-element.41.refs_0_, bf16[48,896]{1,0:T(8,128)(2,1)} %copy-done.13, bf16[48,896]{1,0:T(8,128)(2,1)} %copy-done.14, ...), custom_call_target="tpu_custom_call" | custom-call | tf_op jit(solution)/shard_map/combine/pallas_call | solution.py:245
  (59 shorter events, 3.3 us)
Async XLA Ops:
  8.4 7.9 %collective-permute-start = (bf16[48,896]{1,0:T(8,128)(2,1)}, bf16[48,896]{1,0:T(8,128)(2,1)S(1)}, u32[]{:S(2)}, u32[]{:S(2)}) collective-permute-start(bf16[48,896]{1,0:T(8,128)(2,1)} %get-tuple-element.30), channel_id=1, source_target_pairs={{0,1},{1,0},{2,3},{3,2},{4,5},{5,4},{6,7},{7,6},{8,9},{9,8},{10,11... | collective-permute-start | bytes 258056 | tf_op jit(solution)/shard_map/ppermute | solution.py:158
  8.8 11.1 %collective-permute-start.1 = (bf16[48,896]{1,0:T(8,128)(2,1)}, bf16[48,896]{1,0:T(8,128)(2,1)S(1)}, u32[]{:S(2)}, u32[]{:S(2)}) collective-permute-start(bf16[48,896]{1,0:T(8,128)(2,1)} %get-tuple-element.31), channel_id=1, source_target_pairs={{0,2},{1,3},{2,0},{3,1},{4,6},{5,7},{6,4},{7,5},{8,10},{9,11},{10,... | collective-permute-start | bytes 258056 | tf_op jit(solution)/shard_map/ppermute | solution.py:158
  11.5 9.2 %collective-permute-start.2 = (bf16[48,896]{1,0:T(8,128)(2,1)}, bf16[48,896]{1,0:T(8,128)(2,1)S(1)}, u32[]{:S(2)}, u32[]{:S(2)}) collective-permute-start(bf16[48,896]{1,0:T(8,128)(2,1)} %get-tuple-element.32), channel_id=1, source_target_pairs={{0,3},{1,2},{2,1},{3,0},{4,7},{5,6},{6,5},{7,4},{8,11},{9,10},{10,... | collective-permute-start | bytes 258056 | tf_op jit(solution)/shard_map/ppermute | solution.py:158
  11.5 9.2 %collective-permute-start.3 = (bf16[48,896]{1,0:T(8,128)(2,1)}, bf16[48,896]{1,0:T(8,128)(2,1)S(1)}, u32[]{:S(2)}, u32[]{:S(2)}) collective-permute-start(bf16[48,896]{1,0:T(8,128)(2,1)} %get-tuple-element.33), channel_id=1, source_target_pairs={{0,4},{1,5},{2,6},{3,7},{4,0},{5,1},{6,2},{7,3},{8,12},{9,13},{10,... | collective-permute-start | bytes 258056 | tf_op jit(solution)/shard_map/ppermute | solution.py:158
  14.3 13.1 %collective-permute-start.4 = (bf16[48,896]{1,0:T(8,128)(2,1)}, bf16[48,896]{1,0:T(8,128)(2,1)S(1)}, u32[]{:S(2)}, u32[]{:S(2)}) collective-permute-start(bf16[48,896]{1,0:T(8,128)(2,1)} %get-tuple-element.34), channel_id=1, source_target_pairs={{0,5},{1,4},{2,7},{3,6},{4,1},{5,0},{6,3},{7,2},{8,13},{9,12},{10,... | collective-permute-start | bytes 258056 | tf_op jit(solution)/shard_map/ppermute | solution.py:158
  16.3 11.1 %copy-start.6 = (bf16[48,896]{1,0:T(8,128)(2,1)}, bf16[48,896]{1,0:T(8,128)(2,1)S(1)}, u32[]{:S(2)}) copy-start(bf16[48,896]{1,0:T(8,128)(2,1)S(1)} %collective-permute-done.refs_1_) | copy-start | bytes 258052
  16.3 11.1 %collective-permute-start.5 = (bf16[48,896]{1,0:T(8,128)(2,1)}, bf16[48,896]{1,0:T(8,128)(2,1)S(1)}, u32[]{:S(2)}, u32[]{:S(2)}) collective-permute-start(bf16[48,896]{1,0:T(8,128)(2,1)} %get-tuple-element.35), channel_id=1, source_target_pairs={{0,6},{1,7},{2,4},{3,5},{4,2},{5,3},{6,0},{7,1},{8,14},{9,15},{10,... | collective-permute-start | bytes 258056 | tf_op jit(solution)/shard_map/ppermute | solution.py:158
  20.0 7.5 %copy-start.7 = (bf16[48,896]{1,0:T(8,128)(2,1)}, bf16[48,896]{1,0:T(8,128)(2,1)S(1)}, u32[]{:S(2)}) copy-start(bf16[48,896]{1,0:T(8,128)(2,1)S(1)} %collective-permute-done.1.refs_2_) | copy-start | bytes 258052
  20.0 7.4 %collective-permute-start.6 = (bf16[48,896]{1,0:T(8,128)(2,1)}, bf16[48,896]{1,0:T(8,128)(2,1)S(1)}, u32[]{:S(2)}, u32[]{:S(2)}) collective-permute-start(bf16[48,896]{1,0:T(8,128)(2,1)} %get-tuple-element.36), channel_id=1, source_target_pairs={{0,7},{1,6},{2,5},{3,4},{4,3},{5,2},{6,1},{7,0},{8,15},{9,14},{10,... | collective-permute-start | bytes 258056 | tf_op jit(solution)/shard_map/ppermute | solution.py:158
  20.7 6.7 %copy-start.8 = (bf16[48,896]{1,0:T(8,128)(2,1)}, bf16[48,896]{1,0:T(8,128)(2,1)S(1)}, u32[]{:S(2)}) copy-start(bf16[48,896]{1,0:T(8,128)(2,1)S(1)} %collective-permute-done.2.refs_3_) | copy-start | bytes 258052
  20.7 6.7 %copy-start.9 = (bf16[48,896]{1,0:T(8,128)(2,1)}, bf16[48,896]{1,0:T(8,128)(2,1)S(1)}, u32[]{:S(2)}) copy-start(bf16[48,896]{1,0:T(8,128)(2,1)S(1)} %collective-permute-done.3.refs_4_) | copy-start | bytes 258052
  35.2 12.3 %collective-permute-start.7 = (bf16[2,96,1024]{2,1,0:T(8,128)(2,1)}, bf16[2,96,1024]{2,1,0:T(8,128)(2,1)S(1)}, u32[]{:S(2)}, u32[]{:S(2)}) collective-permute-start(bf16[2,96,1024]{2,1,0:T(8,128)(2,1)} %get-tuple-element.38), channel_id=1, source_target_pairs={{0,8},{8,0},{16,24},{24,16},{1,9},{9,1},{17,25},{25,17},{2,10},{10... | collective-permute-start | bytes 1179656 | tf_op jit(solution)/shard_map/ppermute | solution.py:216
  36.8 19.6 %collective-permute-start.8 = (bf16[2,96,1024]{2,1,0:T(8,128)(2,1)}, bf16[2,96,1024]{2,1,0:T(8,128)(2,1)S(1)}, u32[]{:S(2)}, u32[]{:S(2)}) collective-permute-start(bf16[2,96,1024]{2,1,0:T(8,128)(2,1)} %get-tuple-element.39), channel_id=1, source_target_pairs={{0,16},{8,24},{16,0},{24,8},{1,17},{9,25},{17,1},{25,9},{2,18},{10... | collective-permute-start | bytes 1179656 | tf_op jit(solution)/shard_map/ppermute | solution.py:216
  38.3 18.1 %collective-permute-start.9 = (bf16[2,96,1024]{2,1,0:T(8,128)(2,1)}, bf16[2,96,1024]{2,1,0:T(8,128)(2,1)S(1)}, u32[]{:S(2)}, u32[]{:S(2)}) collective-permute-start(bf16[2,96,1024]{2,1,0:T(8,128)(2,1)} %get-tuple-element.40), channel_id=1, source_target_pairs={{0,24},{8,16},{16,8},{24,0},{1,25},{9,17},{17,9},{25,1},{2,26},{10... | collective-permute-start | bytes 1179656 | tf_op jit(solution)/shard_map/ppermute | solution.py:216
  47.5 8.9 %copy-start = (bf16[2,96,1024]{2,1,0:T(8,128)(2,1)}, bf16[2,96,1024]{2,1,0:T(8,128)(2,1)S(1)}, u32[]{:S(2)}) copy-start(bf16[2,96,1024]{2,1,0:T(8,128)(2,1)S(1)} %collective-permute-done.7.refs_0_) | copy-start | bytes 1179652
  56.4 0.8 copy-start.1
  56.4 0.9 copy-start.2
  59.7 8.9 %collective-permute-start.12 = (bf16[96,1024]{1,0:T(8,128)(2,1)}, bf16[96,1024]{1,0:T(8,128)(2,1)S(1)}, u32[]{:S(2)}, u32[]{:S(2)}) collective-permute-start(bf16[96,1024]{1,0:T(8,128)(2,1)} %hidden.1.refs_0_), channel_id=1, source_target_pairs={{0,24},{8,16},{16,8},{24,0},{1,25},{9,17},{17,9},{25,1},{2,26},{10... | collective-permute-start | bytes 589832 | tf_op jit(solution)/shard_map/ppermute | solution.py:224
  61.2 9.6 %collective-permute-start.11 = (bf16[96,1024]{1,0:T(8,128)(2,1)}, bf16[96,1024]{1,0:T(8,128)(2,1)S(1)}, u32[]{:S(2)}, u32[]{:S(2)}) collective-permute-start(bf16[96,1024]{1,0:T(8,128)(2,1)} %hidden.1.refs_0_), channel_id=1, source_target_pairs={{0,16},{8,24},{16,0},{24,8},{1,17},{9,25},{17,1},{25,9},{2,18},{10... | collective-permute-start | bytes 589832 | tf_op jit(solution)/shard_map/ppermute | solution.py:224
  62.2 8.8 %collective-permute-start.10 = (bf16[96,1024]{1,0:T(8,128)(2,1)}, bf16[96,1024]{1,0:T(8,128)(2,1)S(1)}, u32[]{:S(2)}, u32[]{:S(2)}) collective-permute-start(bf16[96,1024]{1,0:T(8,128)(2,1)} %hidden.1.refs_0_), channel_id=1, source_target_pairs={{0,8},{8,0},{16,24},{24,16},{1,9},{9,1},{17,25},{25,17},{2,10},{10... | collective-permute-start | bytes 589832 | tf_op jit(solution)/shard_map/ppermute | solution.py:224
  68.6 2.4 %copy-start.3 = (bf16[96,1024]{1,0:T(8,128)(2,1)}, bf16[96,1024]{1,0:T(8,128)(2,1)S(1)}, u32[]{:S(2)}) copy-start(bf16[96,1024]{1,0:T(8,128)(2,1)S(1)} %collective-permute-done.12.refs_3_) | copy-start | bytes 589828
  77.1 7.3 %collective-permute-start.13 = (bf16[48,896]{1,0:T(8,128)(2,1)}, bf16[48,896]{1,0:T(8,128)(2,1)S(1)}, u32[]{:S(2)}, u32[]{:S(2)}) collective-permute-start(bf16[48,896]{1,0:T(8,128)(2,1)} %get-tuple-element.42), channel_id=1, source_target_pairs={{0,1},{1,0},{2,3},{3,2},{4,5},{5,4},{6,7},{7,6},{8,9},{9,8},{10,11... | collective-permute-start | bytes 258056 | tf_op jit(solution)/shard_map/ppermute | solution.py:158
  77.1 9.4 %collective-permute-start.14 = (bf16[48,896]{1,0:T(8,128)(2,1)}, bf16[48,896]{1,0:T(8,128)(2,1)S(1)}, u32[]{:S(2)}, u32[]{:S(2)}) collective-permute-start(bf16[48,896]{1,0:T(8,128)(2,1)} %get-tuple-element.43), channel_id=1, source_target_pairs={{0,2},{1,3},{2,0},{3,1},{4,6},{5,7},{6,4},{7,5},{8,10},{9,11},{10,... | collective-permute-start | bytes 258056 | tf_op jit(solution)/shard_map/ppermute | solution.py:158
  81.1 6.9 %collective-permute-start.15 = (bf16[48,896]{1,0:T(8,128)(2,1)}, bf16[48,896]{1,0:T(8,128)(2,1)S(1)}, u32[]{:S(2)}, u32[]{:S(2)}) collective-permute-start(bf16[48,896]{1,0:T(8,128)(2,1)} %get-tuple-element.44), channel_id=1, source_target_pairs={{0,3},{1,2},{2,1},{3,0},{4,7},{5,6},{6,5},{7,4},{8,11},{9,10},{10,... | collective-permute-start | bytes 258056 | tf_op jit(solution)/shard_map/ppermute | solution.py:158
  81.2 6.9 %collective-permute-start.16 = (bf16[48,896]{1,0:T(8,128)(2,1)}, bf16[48,896]{1,0:T(8,128)(2,1)S(1)}, u32[]{:S(2)}, u32[]{:S(2)}) collective-permute-start(bf16[48,896]{1,0:T(8,128)(2,1)} %get-tuple-element.45), channel_id=1, source_target_pairs={{0,4},{1,5},{2,6},{3,7},{4,0},{5,1},{6,2},{7,3},{8,12},{9,13},{10,... | collective-permute-start | bytes 258056 | tf_op jit(solution)/shard_map/ppermute | solution.py:158
  84.4 13.2 %collective-permute-start.17 = (bf16[48,896]{1,0:T(8,128)(2,1)}, bf16[48,896]{1,0:T(8,128)(2,1)S(1)}, u32[]{:S(2)}, u32[]{:S(2)}) collective-permute-start(bf16[48,896]{1,0:T(8,128)(2,1)} %get-tuple-element.46), channel_id=1, source_target_pairs={{0,5},{1,4},{2,7},{3,6},{4,1},{5,0},{6,3},{7,2},{8,13},{9,12},{10,... | collective-permute-start | bytes 258056 | tf_op jit(solution)/shard_map/ppermute | solution.py:158
  84.4 13.2 %copy-start.13 = (bf16[48,896]{1,0:T(8,128)(2,1)}, bf16[48,896]{1,0:T(8,128)(2,1)S(1)}, u32[]{:S(2)}) copy-start(bf16[48,896]{1,0:T(8,128)(2,1)S(1)} %collective-permute-done.13.refs_1_) | copy-start | bytes 258052
  84.4 13.2 %collective-permute-start.18 = (bf16[48,896]{1,0:T(8,128)(2,1)}, bf16[48,896]{1,0:T(8,128)(2,1)S(1)}, u32[]{:S(2)}, u32[]{:S(2)}) collective-permute-start(bf16[48,896]{1,0:T(8,128)(2,1)} %get-tuple-element.47), channel_id=1, source_target_pairs={{0,6},{1,7},{2,4},{3,5},{4,2},{5,3},{6,0},{7,1},{8,14},{9,15},{10,... | collective-permute-start | bytes 258056 | tf_op jit(solution)/shard_map/ppermute | solution.py:158
  86.5 11.1 %copy-start.14 = (bf16[48,896]{1,0:T(8,128)(2,1)}, bf16[48,896]{1,0:T(8,128)(2,1)S(1)}, u32[]{:S(2)}) copy-start(bf16[48,896]{1,0:T(8,128)(2,1)S(1)} %collective-permute-done.14.refs_2_) | copy-start | bytes 258052
  86.5 11.1 %collective-permute-start.19 = (bf16[48,896]{1,0:T(8,128)(2,1)}, bf16[48,896]{1,0:T(8,128)(2,1)S(1)}, u32[]{:S(2)}, u32[]{:S(2)}) collective-permute-start(bf16[48,896]{1,0:T(8,128)(2,1)} %get-tuple-element.48), channel_id=1, source_target_pairs={{0,7},{1,6},{2,5},{3,4},{4,3},{5,2},{6,1},{7,0},{8,15},{9,14},{10,... | collective-permute-start | bytes 258056 | tf_op jit(solution)/shard_map/ppermute | solution.py:158
  88.0 9.6 %copy-start.15 = (bf16[48,896]{1,0:T(8,128)(2,1)}, bf16[48,896]{1,0:T(8,128)(2,1)S(1)}, u32[]{:S(2)}) copy-start(bf16[48,896]{1,0:T(8,128)(2,1)S(1)} %collective-permute-done.15.refs_3_) | copy-start | bytes 258052
  88.1 9.5 %copy-start.16 = (bf16[48,896]{1,0:T(8,128)(2,1)}, bf16[48,896]{1,0:T(8,128)(2,1)S(1)}, u32[]{:S(2)}) copy-start(bf16[48,896]{1,0:T(8,128)(2,1)S(1)} %collective-permute-done.16.refs_4_) | copy-start | bytes 258052
  (8 other events, 5.4 us)

commit v2 on v1

v2 whole, which is shorter than its diff:
```python
import functools

import jax
import jax.numpy as jnp
from jax import lax
from jax.experimental import pallas as pl
from jax.experimental.pallas import tpu as pltpu
from jax.sharding import PartitionSpec as P


BF16 = jnp.bfloat16
F32 = jnp.float32
I32 = jnp.int32
DIRECT_LIMIT = 8


def round_up(n, m):
    return -(-n // m) * m


def slot_room(token_count, top_count, expert_count):
    return max(2, min(token_count // 4, 3 * token_count * top_count // (4 * expert_count)))


def dot(a, b):
    return jnp.dot(a, b, preferred_element_type=F32)


def vmem_specs(n):
    return [pl.BlockSpec(memory_space=pltpu.VMEM)] * n


PARAMS = pltpu.CompilerParams(vmem_limit_bytes=24 * 2**20)


def cost(flops, size):
    return pl.CostEstimate(flops=flops, bytes_accessed=size, transcendentals=0)


SMEM_SPEC = pl.BlockSpec(memory_space=pltpu.SMEM)


def route_kernel(
    sizes, here, place, cap, ids_ref, choice_ref, gate_ref, tok_ref, second, high_ref, low_ref,
    *out_refs
):
    experts, hot, _, half, room_a, room_b = sizes
    top, count = ids_ref.shape
    per = room_a + room_b
    columns = experts * per
    hosting = jnp.int32(0)
    for j in range(hot):
        hosting = jnp.where(place[1, j] == here[1], 1, hosting)
    second[0] = here[2]
    second[1] = hosting
    key = (ids_ref[...] + experts * choice_ref[...]).astype(F32).T
    gate = gate_ref[...].T
    lane = lax.broadcasted_iota(I32, (count, 2 * experts), 1).astype(F32)
    member = jnp.zeros((count, 2 * experts), F32)
    weight = jnp.zeros((count, 2 * experts), F32)
    for k in range(top):
        hit = key[:, k : k + 1] == lane
        member = jnp.where(hit, 1.0, member)
        weight = jnp.where(hit, gate[:, k : k + 1], weight)
    earlier = lax.broadcasted_iota(I32, (count, count), 1) < lax.broadcasted_iota(
        I32, (count, count), 0
    )
    rank = dot(jnp.where(earlier, 1.0, 0.0).astype(BF16), member.astype(BF16))
    lane_row = lax.broadcasted_iota(I32, (1, 2 * experts), 1)
    limit = jnp.zeros((1, 2 * experts), I32)
    for e in range(experts):
        limit = jnp.where(lane_row == e, cap[e], limit)
    for j in range(hot):
        limit = jnp.where(lane_row == place[0, j] + experts, cap[experts + j], limit)
    kept = (member > 0.5) & (rank < limit.astype(F32))
    rank = jnp.where(kept, rank, -1.0)

    column = lax.broadcasted_iota(I32, (1, columns), 1)
    block = jnp.floor((column.astype(F32) + 0.5) * (1.0 / per)).astype(I32)
    slot = column - block * per
    dest = block ^ here[0]
    pair_key = jnp.full((1, columns), -1, I32)
    start = jnp.zeros((1, columns), I32)
    for j in range(hot):
        owner, host = dest == place[0, j], dest == place[1, j]
        pair_key = jnp.where(owner | host, place[0, j] + experts, pair_key)
        start = jnp.where(host, half, start)
    first = slot < room_a
    in_pair = slot - room_a
    wanted = jnp.where(first, dest, jnp.where(in_pair < half, pair_key, -1))
    place_rank = jnp.where(first, slot, in_pair + start).astype(F32)
    spread = jnp.where(
        lax.broadcasted_iota(I32, (2 * experts, columns), 0) == wanted, 1.0, 0.0
    ).astype(BF16)
    chosen = (dot(rank.astype(BF16), spread) == place_rank) & (wanted >= 0)
    weight_high = weight.astype(BF16)
    weight_low = (weight - weight_high.astype(F32)).astype(BF16)
    high_ref[...] = jnp.where(chosen, dot(weight_high, spread), 0.0).astype(BF16)
    low_ref[...] = jnp.where(chosen, dot(weight_low, spread), 0.0).astype(BF16)
    picks = jnp.where(chosen, 1.0, 0.0).T.astype(BF16)
    rows = dot(picks, tok_ref[...]).astype(BF16)
    for i, ref in enumerate(out_refs):
        ref[...] = rows[i * per : (i + 1) * per]


def stage_kernel(at, w_gate, w_up, *refs):
    outs, sems = refs[:-1], refs[-1]
    block = outs[0].shape[2] // 2
    copies = []
    for k, out in enumerate(outs):
        columns = pl.ds(pl.multiple_of((at[0] ^ k) * block, block), block)
        for i, which in enumerate((0, at[1])):
            for g, w in enumerate((w_gate, w_up)):
                copies.append(
                    pltpu.make_async_copy(
                        w.at[0, which, :, columns],
                        out.at[i, :, pl.ds(g * block, block)],
                        sems.at[len(copies)],
                    )
                )
    for copy in copies:
        copy.start()
    for copy in copies:
        copy.wait()


def up_sums(xa, xb, weights, out):
    rows_a = xa.shape[0]
    out[:rows_a] = dot(xa, weights[0]).astype(out.dtype)
    out[rows_a:] = dot(xb, weights[1]).astype(out.dtype)


def up_first_kernel(sizes, *refs):
    experts, room_a, room_b = sizes
    x_refs, weights = refs[:experts], refs[experts]
    out, xa, xb = refs[experts + 1 :]
    for i, ref in enumerate(x_refs):
        xa[i * room_a : (i + 1) * room_a] = ref[:room_a]
        xb[i * room_b : (i + 1) * room_b] = ref[room_a:]
    up_sums(xa[...], xb[...], weights, out)


def up_next_kernel(xa, xb, weights, out):
    up_sums(xa[...], xb[...], weights, out)


def hidden_kernel(own, *refs):
    out = refs[-1]
    block = own.shape[1] // 2
    total = own[...]
    for ref in refs[:-1]:
        total += ref[...].astype(F32)
    out[...] = (jax.nn.silu(total[:, :block]) * total[:, block:]).astype(BF16)


def down_sums(hids, weights, rows_a):
    ra = sum(dot(h[:rows_a], w[0, 0]) for h, w in zip(hids, weights[0::2]))
    rb = sum(dot(h[rows_a:], w[0, 0]) for h, w in zip(hids, weights[1::2]))
    return ra, rb


def down_first_kernel(n, rows_a, at, *refs):
    out = refs[-1]
    out[:rows_a], out[rows_a:] = down_sums(refs[:n], refs[n:-1], rows_a)


def down_last_kernel(n, sizes, at, acc, *refs):
    experts, room_a, room_b = sizes
    rows_a = experts * room_a
    outs = refs[3 * n :]
    ra, rb = down_sums(refs[:n], refs[n : 3 * n], rows_a)
    ra = (ra + acc[:rows_a]).astype(BF16)
    rb = (rb + acc[rows_a:]).astype(BF16)
    for i, out in enumerate(outs):
        out[:room_a] = ra[i * room_a : (i + 1) * room_a]
        out[room_a:] = rb[i * room_b : (i + 1) * room_b]


def combine_kernel(high, low, *refs):
    out, res = refs[-2:]
    per = refs[0].shape[0]
    for i, ref in enumerate(refs[:-2]):
        res[i * per : (i + 1) * per] = ref[...]
    rows = res[...]
    out[...] = (dot(high[...], rows) + dot(low[...], rows)).astype(BF16)


def flips(n, j):
    return [(i, i ^ j) for i in range(n)]


def exchange(pieces, axis):
    n = len(pieces)
    if n > DIRECT_LIMIT:
        moved = lax.all_to_all(jnp.stack(pieces), axis, split_axis=0, concat_axis=0, tiled=True)
        return [moved[i] for i in range(n)]
    moved = [pieces[0]]
    for j in range(1, n):
        moved.append(lax.ppermute(pieces[j], axis, flips(n, j)))
    return moved


def on_device(
    tokens, expert_ids, replica_choice, gate_weights, placement, capacity, w_gate, w_up, w_down
):
    experts = lax.axis_size("expert")
    parts = lax.axis_size("dp")
    me = lax.axis_index("expert").astype(I32)
    count, cols = tokens.shape
    ff = w_gate.shape[3]
    hot = placement.shape[0]
    room = slot_room(count, expert_ids.shape[1], experts)
    half = -(-room // 2)
    room_a, room_b = round_up(room, 16), round_up(half, 16)
    per = room_a + room_b
    flip = me if experts <= DIRECT_LIMIT else jnp.int32(0)
    here = jnp.stack([flip, me, lax.axis_index("dp").astype(I32)])

    sds = jax.ShapeDtypeStruct
    scalars, high, low, *pieces = pl.pallas_call(
        functools.partial(route_kernel, (experts, hot, room, half, room_a, room_b)),
        out_shape=[sds((2,), I32)]
        + [sds((count, experts * per), BF16)] * 2
        + [sds((per, cols), BF16)] * experts,
        in_specs=[SMEM_SPEC] * 3 + vmem_specs(4),
        out_specs=[SMEM_SPEC] + vmem_specs(2 + experts),
        compiler_params=PARAMS,
        name="route",
    )(here, placement.T, capacity, expert_ids.T, replica_choice.T, gate_weights.T, tokens)
    arrived = exchange(pieces, "expert")

    rows_a, rows = experts * room_a, experts * per
    block = ff // parts
    order = list(range(parts - 1, 0, -1)) + [0]
    staged = pl.pallas_call(
        stage_kernel,
        out_shape=[sds((2, cols, 2 * block), BF16)] * parts,
        in_specs=[SMEM_SPEC] + [pl.BlockSpec(memory_space=pl.ANY)] * 2,
        out_specs=vmem_specs(parts),
        scratch_shapes=[pltpu.SemaphoreType.DMA((4 * parts,))],
        compiler_params=PARAMS,
        cost_estimate=cost(0, 16 * cols * ff),
        name="stage",
    )(scalars, w_gate, w_up)

    step = 2 * rows * cols * block
    sums = {}
    for i, k in enumerate(order):
        piece = sds((rows, 2 * block), BF16 if k else F32)
        halves = [sds((rows_a, cols), BF16), sds((rows - rows_a, cols), BF16)]
        made = pl.pallas_call(
            up_next_kernel
            if i
            else functools.partial(up_first_kernel, (experts, room_a, room_b)),
            out_shape=[piece] + ([] if i else halves),
            in_specs=vmem_specs(3 if i else experts + 1),
            out_specs=vmem_specs(1 if i else 3),
            compiler_params=PARAMS,
            cost_estimate=cost(2 * step, rows * (cols + 2 * block) * 2),
            name="up",
        )(*([xa, xb] if i else arrived), staged[k])
        sums[k] = made[0]
        if not i:
            xa, xb = made[1:]
        if k:
            sums[k] = lax.ppermute(sums[k], "dp", flips(parts, k))
    hidden = pl.pallas_call(
        hidden_kernel,
        out_shape=sds((rows, block), BF16),
        in_specs=vmem_specs(parts),
        out_specs=vmem_specs(1)[0],
        compiler_params=PARAMS,
        name="hidden",
    )(*[sums[k] for k in range(parts)])
    spread = {0: hidden}
    for k in order[:-1]:
        spread[k] = lax.ppermute(hidden, "dp", flips(parts, k))

    def down(kernel, k_list, operands, out_shape):
        specs = [pl.BlockSpec(x.shape, lambda f, s: (0, 0)) for x in operands]
        for k in k_list:
            for i in range(2):
                pick = lambda f, s, k=k, i=i: (0, s[1] * i, s[0] ^ k, 0)
                specs.append(pl.BlockSpec((1, 1, block, cols), pick))
        return pl.pallas_call(
            kernel,
            out_shape=out_shape,
            grid_spec=pltpu.PrefetchScalarGridSpec(
                num_scalar_prefetch=1,
                grid=(1,),
                in_specs=specs,
                out_specs=[pl.BlockSpec(x.shape, lambda f, s: (0, 0)) for x in out_shape],
            ),
            compiler_params=PARAMS,
            cost_estimate=cost(len(k_list) * step, rows * cols * 4),
            name="down",
        )(scalars, *operands, *([w_down] * (2 * len(k_list))))

    early, late = list(range(parts - 1)), [parts - 1]
    (acc,) = down(
        functools.partial(down_first_kernel, len(early), rows_a),
        early,
        [spread[k] for k in early],
        [sds((rows, cols), F32)],
    )
    results = down(
        functools.partial(down_last_kernel, len(late), (experts, room_a, room_b)),
        late,
        [acc] + [spread[k] for k in late],
        [sds((per, cols), BF16)] * experts,
    )
    returned = exchange(results, "expert")
    return pl.pallas_call(
        combine_kernel,
        out_shape=sds((count, cols), BF16),
        in_specs=vmem_specs(2 + experts),
        out_specs=vmem_specs(1)[0],
        scratch_shapes=[pltpu.VMEM((experts * per, cols), BF16)],
        compiler_params=PARAMS,
        name="combine",
    )(high, low, *returned)


def solution(mesh):
    return jax.shard_map(
        on_device,
        mesh=mesh,
        in_specs=(
            P("expert", "dp"),
            P("expert", None),
            P("expert", None),
            P("expert", None),
            P(),
            P(),
            P("expert", None, "dp", None),
            P("expert", None, "dp", None),
            P("expert", None, None, "dp"),
        ),
        out_specs=P("expert", "dp"),
        check_vma=False,
    )
```

time: 103 us -> 84.5 us (0.82)
  the two profiles are of different devices: /device:TPU:0 before, /device:TPU:15 now
where the time goes in v2:
time: 84.5 us; the launch traced here: 84.2 us
  waiting for transfers between devices  44.6 us (53%)
  starting transfers between devices  21.2 us (25%)
  Pallas kernels  9.73 us (12%)
  local copies, waits for them, and re-layouts  8.41 us (10%)
    ppermute x14, waiting for transfers between devices, exchange(): moved.append(lax.ppermute(pieces[j], axis, flips(n, j)))  20.4 us
    ppermute x3, waiting for transfers between devices, on_device(): sums[k] = lax.ppermute(sums[k], 'dp', flips(parts, k))  17.1 us
    ppermute x14, starting transfers between devices, exchange(): moved.append(lax.ppermute(pieces[j], axis, flips(n, j)))  15.8 us
    unnamed x18, local copies, waits for them, and re-layouts  8.41 us
    ppermute x3, waiting for transfers between devices, on_device(): spread[k] = lax.ppermute(hidden, 'dp', flips(parts, k))  7.1 us
    ppermute x3, starting transfers between devices, on_device(): spread[k] = lax.ppermute(hidden, 'dp', flips(parts, k))  2.71 us
    ppermute x3, starting transfers between devices, on_device(): sums[k] = lax.ppermute(sums[k], 'dp', flips(parts, k))  2.71 us
    pallas_call x4, Pallas kernels, on_device(): pl.pallas_call(up_next_kernel if i else functools.partial(up_first_kernel...  2.31 us
  transfers between devices with their start and end apart: 20, of which 13 were waited for; matrix products, arithmetic and copies ran while one was open for 0% of the time, Pallas kernels for 4%

profile of v2, /device:TPU:15, one launch (start us, length us, event | category | flops | bytes accessed | tf_op | source)
XLA Modules:
  0.0 84.2 jit_solution(5093986507599902949)
XLA Ops:
  0.1 0.9 %copy-done.3 = bf16[128,896]{1,0:T(8,128)(2,1)S(1)} copy-done((bf16[128,896]{1,0:T(8,128)(2,1)S(1)}, bf16[128,896]{1,0:T(8,128)(2,1)}, u32[]{:S(2)}) %copy-start.3) | copy-done | bytes 229400
  4.4 2.1 %route.1 = (s32[2]{0:T(128)S(1)}, bf16[128,384]{1,0:T(8,128)(2,1)S(1)}, bf16[128,384]{1,0:T(8,128)(2,1)S(1)}, bf16[48,896]{1,0:T(8,128)(2,1)S(1)}, bf16[48,896]{...) custom-call(s32[3]{0:T(128)S(1)} %pad_add_fusion.here, ...), custom_call_target="tpu_custom_call" | custom-call | tf_op jit(solution)/shard_map/route/pallas_call | solution.py:220
  7.5 1.5 %collective-permute-start.2 = (bf16[48,896]{1,0:T(8,128)(2,1)S(1)}, bf16[48,896]{1,0:T(8,128)(2,1)S(1)}, u32[]{:S(2)}, u32[]{:S(2)}) collective-permute-start(bf16[48,896]{1,0:T(8,128)(2,1)S(1)} %get-tuple-element.37), channel_id=1, source_target_pairs={{0,3},{1,2},{2,1},{3,0},{4,7},{5,6},{6,5},{7,4},{8,11},{9,10},{10,... | collective-permute-start | bytes 258056 | tf_op jit(solution)/shard_map/ppermute | solution.py:199
  9.0 2.3 %collective-permute-start.3 = (bf16[48,896]{1,0:T(8,128)(2,1)S(1)}, bf16[48,896]{1,0:T(8,128)(2,1)S(1)}, u32[]{:S(2)}, u32[]{:S(2)}) collective-permute-start(bf16[48,896]{1,0:T(8,128)(2,1)S(1)} %get-tuple-element.38), channel_id=1, source_target_pairs={{0,4},{1,5},{2,6},{3,7},{4,0},{5,1},{6,2},{7,3},{8,12},{9,13},{10,... | collective-permute-start | bytes 258056 | tf_op jit(solution)/shard_map/ppermute | solution.py:199
  11.7 1.3 %collective-permute-start.5 = (bf16[48,896]{1,0:T(8,128)(2,1)S(1)}, bf16[48,896]{1,0:T(8,128)(2,1)S(1)}, u32[]{:S(2)}, u32[]{:S(2)}) collective-permute-start(bf16[48,896]{1,0:T(8,128)(2,1)S(1)} %get-tuple-element.40), channel_id=1, source_target_pairs={{0,6},{1,7},{2,4},{3,5},{4,2},{5,3},{6,0},{7,1},{8,14},{9,15},{10,... | collective-permute-start | bytes 258056 | tf_op jit(solution)/shard_map/ppermute | solution.py:199
  13.7 2.0 %copy-done.1 = bf16[1,2,896,1024]{3,2,1,0:T(8,128)(2,1)S(1)} copy-done((bf16[1,2,896,1024]{3,2,1,0:T(8,128)(2,1)S(1)}, bf16[1,2,896,1024]{3,2,1,0:T(8,128)(2,1)}, u32[]{:S(2)}) %copy-start.1) | copy-done | bytes 3670040
  15.8 2.0 %copy-done.2 = bf16[1,2,896,1024]{3,2,1,0:T(8,128)(2,1)S(1)} copy-done((bf16[1,2,896,1024]{3,2,1,0:T(8,128)(2,1)S(1)}, bf16[1,2,896,1024]{3,2,1,0:T(8,128)(2,1)}, u32[]{:S(2)}) %copy-start.2) | copy-done | bytes 3670040
  17.8 1.7 %stage.1 = (bf16[2,896,512]{2,1,0:T(8,128)(2,1)S(1)}, bf16[2,896,512]{2,1,0:T(8,128)(2,1)S(1)}, bf16[2,896,512]{2,1,0:T(8,128)(2,1)S(1)}, bf16[2,896,512]{2,1,0:T(8,128)(2,1)S(1)}) custom-call(s32[2]{0:T(128)S(1)} %get-tuple-element.33.at, bf16[1,2,896,1024]{3,2,1,0:T(8,128)(2,1)S(1)} %copy-done.1, bf16[1,2,896,1024]{3,2,1,0:T(8,128)(2,1)S(1)} %copy-done.2), custom_call_target="tpu_custom_call" | custom-call | bytes 14680064 | tf_op jit(solution)/shard_map/stage/pallas_call | solution.py:235
  19.5 0.9 %collective-permute-done.3.refs_4_ = bf16[48,896]{1,0:T(8,128)(2,1)S(1)} collective-permute-done((bf16[48,896]{1,0:T(8,128)(2,1)S(1)}, bf16[48,896]{1,0:T(8,128)(2,1)S(1)}, u32[]{:S(2)}, u32[]{:S(2)}) %collective-permute-start.3) | collective-permute-done | bytes 86048 | tf_op jit(solution)/shard_map/ppermute | solution.py:199
  20.4 2.0 %collective-permute-done.4.refs_5_ = bf16[48,896]{1,0:T(8,128)(2,1)S(1)} collective-permute-done((bf16[48,896]{1,0:T(8,128)(2,1)S(1)}, bf16[48,896]{1,0:T(8,128)(2,1)S(1)}, u32[]{:S(2)}, u32[]{:S(2)}) %collective-permute-start.4) | collective-permute-done | bytes 86048 | tf_op jit(solution)/shard_map/ppermute | solution.py:199
  22.4 2.6 %collective-permute-done.5.refs_6_ = bf16[48,896]{1,0:T(8,128)(2,1)S(1)} collective-permute-done((bf16[48,896]{1,0:T(8,128)(2,1)S(1)}, bf16[48,896]{1,0:T(8,128)(2,1)S(1)}, u32[]{:S(2)}, u32[]{:S(2)}) %collective-permute-start.5) | collective-permute-done | bytes 86048 | tf_op jit(solution)/shard_map/ppermute | solution.py:199
  25.1 1.8 %collective-permute-done.6.refs_7_ = bf16[48,896]{1,0:T(8,128)(2,1)S(1)} collective-permute-done((bf16[48,896]{1,0:T(8,128)(2,1)S(1)}, bf16[48,896]{1,0:T(8,128)(2,1)S(1)}, u32[]{:S(2)}, u32[]{:S(2)}) %collective-permute-start.6) | collective-permute-done | bytes 86048 | tf_op jit(solution)/shard_map/ppermute | solution.py:199
  28.9 1.2 %collective-permute-start.7 = (bf16[384,512]{1,0:T(8,128)(2,1)S(1)}, bf16[384,512]{1,0:T(8,128)(2,1)S(1)}, u32[]{:S(2)}, u32[]{:S(2)}) collective-permute-start(bf16[384,512]{1,0:T(8,128)(2,1)S(1)} %up.6), channel_id=1, source_target_pairs={{0,8},{8,0},{16,24},{24,16},{1,9},{9,1},{17,25},{25,17},{2,10},{10... | collective-permute-start | bytes 1179656 | tf_op jit(solution)/shard_map/ppermute | solution.py:266
  30.2 1.2 %collective-permute-start.8 = (bf16[384,512]{1,0:T(8,128)(2,1)S(1)}, bf16[384,512]{1,0:T(8,128)(2,1)S(1)}, u32[]{:S(2)}, u32[]{:S(2)}) collective-permute-start(bf16[384,512]{1,0:T(8,128)(2,1)S(1)} %up.7), channel_id=1, source_target_pairs={{0,16},{8,24},{16,0},{24,8},{1,17},{9,25},{17,1},{25,9},{2,18},{10... | collective-permute-start | bytes 1179656 | tf_op jit(solution)/shard_map/ppermute | solution.py:266
  32.0 8.0 %collective-permute-done.9.refs_2_ = bf16[384,512]{1,0:T(8,128)(2,1)S(1)} collective-permute-done((bf16[384,512]{1,0:T(8,128)(2,1)S(1)}, bf16[384,512]{1,0:T(8,128)(2,1)S(1)}, u32[]{:S(2)}, u32[]{:S(2)}) %collective-permute-start.9) | collective-permute-done | bytes 393248 | tf_op jit(solution)/shard_map/ppermute | solution.py:266
  40.0 7.5 %collective-permute-done.7.refs_0_ = bf16[384,512]{1,0:T(8,128)(2,1)S(1)} collective-permute-done((bf16[384,512]{1,0:T(8,128)(2,1)S(1)}, bf16[384,512]{1,0:T(8,128)(2,1)S(1)}, u32[]{:S(2)}, u32[]{:S(2)}) %collective-permute-start.7) | collective-permute-done | bytes 393248 | tf_op jit(solution)/shard_map/ppermute | solution.py:266
  47.4 1.7 %collective-permute-done.8.refs_1_ = bf16[384,512]{1,0:T(8,128)(2,1)S(1)} collective-permute-done((bf16[384,512]{1,0:T(8,128)(2,1)S(1)}, bf16[384,512]{1,0:T(8,128)(2,1)S(1)}, u32[]{:S(2)}, u32[]{:S(2)}) %collective-permute-start.8) | collective-permute-done | bytes 393248 | tf_op jit(solution)/shard_map/ppermute | solution.py:266
  49.9 2.2 %collective-permute-start.12 = (bf16[384,256]{1,0:T(8,128)(2,1)S(1)}, bf16[384,256]{1,0:T(8,128)(2,1)S(1)}, u32[]{:S(2)}, u32[]{:S(2)}) collective-permute-start(bf16[384,256]{1,0:T(8,128)(2,1)S(1)} %hidden.1.refs_0_), channel_id=1, source_target_pairs={{0,24},{8,16},{16,8},{24,0},{1,25},{9,17},{17,9},{25,1},{2,26},{10... | collective-permute-start | bytes 589832 | tf_op jit(solution)/shard_map/ppermute | solution.py:277
  52.0 3.3 %collective-permute-done.11.refs_2_ = bf16[384,256]{1,0:T(8,128)(2,1)S(1)} collective-permute-done((bf16[384,256]{1,0:T(8,128)(2,1)S(1)}, bf16[384,256]{1,0:T(8,128)(2,1)S(1)}, u32[]{:S(2)}, u32[]{:S(2)}) %collective-permute-start.11) | collective-permute-done | bytes 196640 | tf_op jit(solution)/shard_map/ppermute | solution.py:277
  55.4 1.3 %down.2.acc = f32[384,896]{1,0:T(8,128)S(1)} custom-call(s32[2]{0:T(128)S(1)} %get-tuple-element.33.at, bf16[384,256]{1,0:T(8,128)(2,1)S(1)} %hidden.1.refs_0_, bf16[384,256]{1,0:T(8,128)(2,1)S(1)} %collective-permute-done.10.refs_1_, bf16[384,256]{1,0:T(8,128)(2,1)S(1)} %collective-permute-done.11.refs_2_, bf16[1,2,1024,896]{3,2,1,0:T(8,128)(2,1)S(1)} %copy-done, ...), custom_call_target="tpu_custom_call" | custom-call | flops 528482304 | bytes 1376256 | tf_op jit(solution)/shard_map/down/pallas_call | solution.py:285
  56.7 3.8 %collective-permute-done.12.refs_0_ = bf16[384,256]{1,0:T(8,128)(2,1)S(1)} collective-permute-done((bf16[384,256]{1,0:T(8,128)(2,1)S(1)}, bf16[384,256]{1,0:T(8,128)(2,1)S(1)}, u32[]{:S(2)}, u32[]{:S(2)}) %collective-permute-start.12) | collective-permute-done | bytes 196640 | tf_op jit(solution)/shard_map/ppermute | solution.py:277
  61.4 1.7 %collective-permute-start.13 = (bf16[48,896]{1,0:T(8,128)(2,1)S(1)}, bf16[48,896]{1,0:T(8,128)(2,1)S(1)}, u32[]{:S(2)}, u32[]{:S(2)}) collective-permute-start(bf16[48,896]{1,0:T(8,128)(2,1)S(1)} %get-tuple-element.50), channel_id=1, source_target_pairs={{0,1},{1,0},{2,3},{3,2},{4,5},{5,4},{6,7},{7,6},{8,9},{9,8},{10,11... | collective-permute-start | bytes 258056 | tf_op jit(solution)/shard_map/ppermute | solution.py:199
  63.1 1.7 %collective-permute-start.15 = (bf16[48,896]{1,0:T(8,128)(2,1)S(1)}, bf16[48,896]{1,0:T(8,128)(2,1)S(1)}, u32[]{:S(2)}, u32[]{:S(2)}) collective-permute-start(bf16[48,896]{1,0:T(8,128)(2,1)S(1)} %get-tuple-element.52), channel_id=1, source_target_pairs={{0,3},{1,2},{2,1},{3,0},{4,7},{5,6},{6,5},{7,4},{8,11},{9,10},{10,... | collective-permute-start | bytes 258056 | tf_op jit(solution)/shard_map/ppermute | solution.py:199
  64.8 1.1 %collective-permute-start.16 = (bf16[48,896]{1,0:T(8,128)(2,1)S(1)}, bf16[48,896]{1,0:T(8,128)(2,1)S(1)}, u32[]{:S(2)}, u32[]{:S(2)}) collective-permute-start(bf16[48,896]{1,0:T(8,128)(2,1)S(1)} %get-tuple-element.53), channel_id=1, source_target_pairs={{0,4},{1,5},{2,6},{3,7},{4,0},{5,1},{6,2},{7,3},{8,12},{9,13},{10,... | collective-permute-start | bytes 258056 | tf_op jit(solution)/shard_map/ppermute | solution.py:199
  65.9 1.6 %collective-permute-start.17 = (bf16[48,896]{1,0:T(8,128)(2,1)S(1)}, bf16[48,896]{1,0:T(8,128)(2,1)S(1)}, u32[]{:S(2)}, u32[]{:S(2)}) collective-permute-start(bf16[48,896]{1,0:T(8,128)(2,1)S(1)} %get-tuple-element.54), channel_id=1, source_target_pairs={{0,5},{1,4},{2,7},{3,6},{4,1},{5,0},{6,3},{7,2},{8,13},{9,12},{10,... | collective-permute-start | bytes 258056 | tf_op jit(solution)/shard_map/ppermute | solution.py:199
  67.5 1.6 %collective-permute-start.18 = (bf16[48,896]{1,0:T(8,128)(2,1)S(1)}, bf16[48,896]{1,0:T(8,128)(2,1)S(1)}, u32[]{:S(2)}, u32[]{:S(2)}) collective-permute-start(bf16[48,896]{1,0:T(8,128)(2,1)S(1)} %get-tuple-element.55), channel_id=1, source_target_pairs={{0,6},{1,7},{2,4},{3,5},{4,2},{5,3},{6,0},{7,1},{8,14},{9,15},{10,... | collective-permute-start | bytes 258056 | tf_op jit(solution)/shard_map/ppermute | solution.py:199
  69.1 1.0 %collective-permute-start.19 = (bf16[48,896]{1,0:T(8,128)(2,1)S(1)}, bf16[48,896]{1,0:T(8,128)(2,1)S(1)}, u32[]{:S(2)}, u32[]{:S(2)}) collective-permute-start(bf16[48,896]{1,0:T(8,128)(2,1)S(1)} %get-tuple-element.56), channel_id=1, source_target_pairs={{0,7},{1,6},{2,5},{3,4},{4,3},{5,2},{6,1},{7,0},{8,15},{9,14},{10,... | collective-permute-start | bytes 258056 | tf_op jit(solution)/shard_map/ppermute | solution.py:199
  70.0 2.0 %collective-permute-done.16.refs_4_ = bf16[48,896]{1,0:T(8,128)(2,1)S(1)} collective-permute-done((bf16[48,896]{1,0:T(8,128)(2,1)S(1)}, bf16[48,896]{1,0:T(8,128)(2,1)S(1)}, u32[]{:S(2)}, u32[]{:S(2)}) %collective-permute-start.16) | collective-permute-done | bytes 86048 | tf_op jit(solution)/shard_map/ppermute | solution.py:199
  72.1 5.1 %collective-permute-done.17.refs_5_ = bf16[48,896]{1,0:T(8,128)(2,1)S(1)} collective-permute-done((bf16[48,896]{1,0:T(8,128)(2,1)S(1)}, bf16[48,896]{1,0:T(8,128)(2,1)S(1)}, u32[]{:S(2)}, u32[]{:S(2)}) %collective-permute-start.17) | collective-permute-done | bytes 86048 | tf_op jit(solution)/shard_map/ppermute | solution.py:199
  77.2 4.0 %collective-permute-done.18.refs_6_ = bf16[48,896]{1,0:T(8,128)(2,1)S(1)} collective-permute-done((bf16[48,896]{1,0:T(8,128)(2,1)S(1)}, bf16[48,896]{1,0:T(8,128)(2,1)S(1)}, u32[]{:S(2)}, u32[]{:S(2)}) %collective-permute-start.18) | collective-permute-done | bytes 86048 | tf_op jit(solution)/shard_map/ppermute | solution.py:199
  81.2 1.8 %collective-permute-done.19.refs_7_ = bf16[48,896]{1,0:T(8,128)(2,1)S(1)} collective-permute-done((bf16[48,896]{1,0:T(8,128)(2,1)S(1)}, bf16[48,896]{1,0:T(8,128)(2,1)S(1)}, u32[]{:S(2)}, u32[]{:S(2)}) %collective-permute-start.19) | collective-permute-done | bytes 86048 | tf_op jit(solution)/shard_map/ppermute | solution.py:199
  83.0 1.1 %combine.1 = bf16[128,896]{1,0:T(8,128)(2,1)} custom-call(bf16[128,384]{1,0:T(8,128)(2,1)S(1)} %get-tuple-element.31.high, bf16[128,384]{1,0:T(8,128)(2,1)S(1)} %get-tuple-element.32.low, bf16[48,896]{1,0:T(8,128)(2,1)S(1)} %get-tuple-element.49.refs_0_, bf16[48,896]{1,0:T(8,128)(2,1)S(1)} %collective-permute-done.13.refs_1_, ...), custom_call_target="tpu_custom_call" | custom-call | tf_op jit(solution)/shard_map/combine/pallas_call | solution.py:313
  (37 shorter events, 9.7 us)
Async XLA Ops:
  0.1 0.9 %copy-start.3 = (bf16[128,896]{1,0:T(8,128)(2,1)S(1)}, bf16[128,896]{1,0:T(8,128)(2,1)}, u32[]{:S(2)}) copy-start(bf16[128,896]{1,0:T(8,128)(2,1)} %tok_ref.1) | copy-start | bytes 688132
  1.0 0.7 copy-start.4
  1.7 0.7 copy-start.5
  2.4 0.7 copy-start.6
  3.1 0.7 copy-start.7
  3.8 0.7 copy-start.8
  6.6 5.1 %collective-permute-start = (bf16[48,896]{1,0:T(8,128)(2,1)S(1)}, bf16[48,896]{1,0:T(8,128)(2,1)S(1)}, u32[]{:S(2)}, u32[]{:S(2)}) collective-permute-start(bf16[48,896]{1,0:T(8,128)(2,1)S(1)} %get-tuple-element.35), channel_id=1, source_target_pairs={{0,1},{1,0},{2,3},{3,2},{4,5},{5,4},{6,7},{7,6},{8,9},{9,8},{10,11... | collective-permute-start | bytes 258056 | tf_op jit(solution)/shard_map/ppermute | solution.py:199
  7.3 5.7 %collective-permute-start.1 = (bf16[48,896]{1,0:T(8,128)(2,1)S(1)}, bf16[48,896]{1,0:T(8,128)(2,1)S(1)}, u32[]{:S(2)}, u32[]{:S(2)}) collective-permute-start(bf16[48,896]{1,0:T(8,128)(2,1)S(1)} %get-tuple-element.36), channel_id=1, source_target_pairs={{0,2},{1,3},{2,0},{3,1},{4,6},{5,7},{6,4},{7,5},{8,10},{9,11},{10,... | collective-permute-start | bytes 258056 | tf_op jit(solution)/shard_map/ppermute | solution.py:199
  7.5 12.1 %collective-permute-start.2 = (bf16[48,896]{1,0:T(8,128)(2,1)S(1)}, bf16[48,896]{1,0:T(8,128)(2,1)S(1)}, u32[]{:S(2)}, u32[]{:S(2)}) collective-permute-start(bf16[48,896]{1,0:T(8,128)(2,1)S(1)} %get-tuple-element.37), channel_id=1, source_target_pairs={{0,3},{1,2},{2,1},{3,0},{4,7},{5,6},{6,5},{7,4},{8,11},{9,10},{10,... | collective-permute-start | bytes 258056 | tf_op jit(solution)/shard_map/ppermute | solution.py:199
  9.0 11.4 %collective-permute-start.3 = (bf16[48,896]{1,0:T(8,128)(2,1)S(1)}, bf16[48,896]{1,0:T(8,128)(2,1)S(1)}, u32[]{:S(2)}, u32[]{:S(2)}) collective-permute-start(bf16[48,896]{1,0:T(8,128)(2,1)S(1)} %get-tuple-element.38), channel_id=1, source_target_pairs={{0,4},{1,5},{2,6},{3,7},{4,0},{5,1},{6,2},{7,3},{8,12},{9,13},{10,... | collective-permute-start | bytes 258056 | tf_op jit(solution)/shard_map/ppermute | solution.py:199
  11.3 11.1 %collective-permute-start.4 = (bf16[48,896]{1,0:T(8,128)(2,1)S(1)}, bf16[48,896]{1,0:T(8,128)(2,1)S(1)}, u32[]{:S(2)}, u32[]{:S(2)}) collective-permute-start(bf16[48,896]{1,0:T(8,128)(2,1)S(1)} %get-tuple-element.39), channel_id=1, source_target_pairs={{0,5},{1,4},{2,7},{3,6},{4,1},{5,0},{6,3},{7,2},{8,13},{9,12},{10,... | collective-permute-start | bytes 258056 | tf_op jit(solution)/shard_map/ppermute | solution.py:199
  11.7 13.4 %collective-permute-start.5 = (bf16[48,896]{1,0:T(8,128)(2,1)S(1)}, bf16[48,896]{1,0:T(8,128)(2,1)S(1)}, u32[]{:S(2)}, u32[]{:S(2)}) collective-permute-start(bf16[48,896]{1,0:T(8,128)(2,1)S(1)} %get-tuple-element.40), channel_id=1, source_target_pairs={{0,6},{1,7},{2,4},{3,5},{4,2},{5,3},{6,0},{7,1},{8,14},{9,15},{10,... | collective-permute-start | bytes 258056 | tf_op jit(solution)/shard_map/ppermute | solution.py:199
  13.0 13.9 %collective-permute-start.6 = (bf16[48,896]{1,0:T(8,128)(2,1)S(1)}, bf16[48,896]{1,0:T(8,128)(2,1)S(1)}, u32[]{:S(2)}, u32[]{:S(2)}) collective-permute-start(bf16[48,896]{1,0:T(8,128)(2,1)S(1)} %get-tuple-element.41), channel_id=1, source_target_pairs={{0,7},{1,6},{2,5},{3,4},{4,3},{5,2},{6,1},{7,0},{8,15},{9,14},{10,... | collective-permute-start | bytes 258056 | tf_op jit(solution)/shard_map/ppermute | solution.py:199
  13.7 2.0 %copy-start.1 = (bf16[1,2,896,1024]{3,2,1,0:T(8,128)(2,1)S(1)}, bf16[1,2,896,1024]{3,2,1,0:T(8,128)(2,1)}, u32[]{:S(2)}) copy-start(bf16[1,2,896,1024]{3,2,1,0:T(8,128)(2,1)} %w_gate.1) | copy-start | bytes 11010052
  15.8 2.0 %copy-start.2 = (bf16[1,2,896,1024]{3,2,1,0:T(8,128)(2,1)S(1)}, bf16[1,2,896,1024]{3,2,1,0:T(8,128)(2,1)}, u32[]{:S(2)}) copy-start(bf16[1,2,896,1024]{3,2,1,0:T(8,128)(2,1)} %w_up.1) | copy-start | bytes 11010052
  28.7 11.3 %collective-permute-start.9 = (bf16[384,512]{1,0:T(8,128)(2,1)S(1)}, bf16[384,512]{1,0:T(8,128)(2,1)S(1)}, u32[]{:S(2)}, u32[]{:S(2)}) collective-permute-start(bf16[384,512]{1,0:T(8,128)(2,1)S(1)} %get-tuple-element.48), channel_id=1, source_target_pairs={{0,24},{8,16},{16,8},{24,0},{1,25},{9,17},{17,9},{25,1},{2,26},{10... | collective-permute-start | bytes 1179656 | tf_op jit(solution)/shard_map/ppermute | solution.py:266
  28.9 18.5 %collective-permute-start.7 = (bf16[384,512]{1,0:T(8,128)(2,1)S(1)}, bf16[384,512]{1,0:T(8,128)(2,1)S(1)}, u32[]{:S(2)}, u32[]{:S(2)}) collective-permute-start(bf16[384,512]{1,0:T(8,128)(2,1)S(1)} %up.6), channel_id=1, source_target_pairs={{0,8},{8,0},{16,24},{24,16},{1,9},{9,1},{17,25},{25,17},{2,10},{10... | collective-permute-start | bytes 1179656 | tf_op jit(solution)/shard_map/ppermute | solution.py:266
  30.2 18.9 %collective-permute-start.8 = (bf16[384,512]{1,0:T(8,128)(2,1)S(1)}, bf16[384,512]{1,0:T(8,128)(2,1)S(1)}, u32[]{:S(2)}, u32[]{:S(2)}) collective-permute-start(bf16[384,512]{1,0:T(8,128)(2,1)S(1)} %up.7), channel_id=1, source_target_pairs={{0,16},{8,24},{16,0},{24,8},{1,17},{9,25},{17,1},{25,9},{2,18},{10... | collective-permute-start | bytes 1179656 | tf_op jit(solution)/shard_map/ppermute | solution.py:266
  31.4 24.0 %copy-start = (bf16[1,2,1024,896]{3,2,1,0:T(8,128)(2,1)S(1)}, bf16[1,2,1024,896]{3,2,1,0:T(8,128)(2,1)}, u32[]{:S(2)}) copy-start(bf16[1,2,1024,896]{3,2,1,0:T(8,128)(2,1)} %refs_2_.1) | copy-start | bytes 11010052
  49.3 6.0 %collective-permute-start.11 = (bf16[384,256]{1,0:T(8,128)(2,1)S(1)}, bf16[384,256]{1,0:T(8,128)(2,1)S(1)}, u32[]{:S(2)}, u32[]{:S(2)}) collective-permute-start(bf16[384,256]{1,0:T(8,128)(2,1)S(1)} %hidden.1.refs_0_), channel_id=1, source_target_pairs={{0,16},{8,24},{16,0},{24,8},{1,17},{9,25},{17,1},{25,9},{2,18},{10... | collective-permute-start | bytes 589832 | tf_op jit(solution)/shard_map/ppermute | solution.py:277
  49.6 5.7 %collective-permute-start.10 = (bf16[384,256]{1,0:T(8,128)(2,1)S(1)}, bf16[384,256]{1,0:T(8,128)(2,1)S(1)}, u32[]{:S(2)}, u32[]{:S(2)}) collective-permute-start(bf16[384,256]{1,0:T(8,128)(2,1)S(1)} %hidden.1.refs_0_), channel_id=1, source_target_pairs={{0,8},{8,0},{16,24},{24,16},{1,9},{9,1},{17,25},{25,17},{2,10},{10... | collective-permute-start | bytes 589832 | tf_op jit(solution)/shard_map/ppermute | solution.py:277
  49.9 10.6 %collective-permute-start.12 = (bf16[384,256]{1,0:T(8,128)(2,1)S(1)}, bf16[384,256]{1,0:T(8,128)(2,1)S(1)}, u32[]{:S(2)}, u32[]{:S(2)}) collective-permute-start(bf16[384,256]{1,0:T(8,128)(2,1)S(1)} %hidden.1.refs_0_), channel_id=1, source_target_pairs={{0,24},{8,16},{16,8},{24,0},{1,25},{9,17},{17,9},{25,1},{2,26},{10... | collective-permute-start | bytes 589832 | tf_op jit(solution)/shard_map/ppermute | solution.py:277
  61.4 6.1 %collective-permute-start.13 = (bf16[48,896]{1,0:T(8,128)(2,1)S(1)}, bf16[48,896]{1,0:T(8,128)(2,1)S(1)}, u32[]{:S(2)}, u32[]{:S(2)}) collective-permute-start(bf16[48,896]{1,0:T(8,128)(2,1)S(1)} %get-tuple-element.50), channel_id=1, source_target_pairs={{0,1},{1,0},{2,3},{3,2},{4,5},{5,4},{6,7},{7,6},{8,9},{9,8},{10,11... | collective-permute-start | bytes 258056 | tf_op jit(solution)/shard_map/ppermute | solution.py:199
  63.1 6.0 %collective-permute-start.14 = (bf16[48,896]{1,0:T(8,128)(2,1)S(1)}, bf16[48,896]{1,0:T(8,128)(2,1)S(1)}, u32[]{:S(2)}, u32[]{:S(2)}) collective-permute-start(bf16[48,896]{1,0:T(8,128)(2,1)S(1)} %get-tuple-element.51), channel_id=1, source_target_pairs={{0,2},{1,3},{2,0},{3,1},{4,6},{5,7},{6,4},{7,5},{8,10},{9,11},{10,... | collective-permute-start | bytes 258056 | tf_op jit(solution)/shard_map/ppermute | solution.py:199
  63.1 6.9 %collective-permute-start.15 = (bf16[48,896]{1,0:T(8,128)(2,1)S(1)}, bf16[48,896]{1,0:T(8,128)(2,1)S(1)}, u32[]{:S(2)}, u32[]{:S(2)}) collective-permute-start(bf16[48,896]{1,0:T(8,128)(2,1)S(1)} %get-tuple-element.52), channel_id=1, source_target_pairs={{0,3},{1,2},{2,1},{3,0},{4,7},{5,6},{6,5},{7,4},{8,11},{9,10},{10,... | collective-permute-start | bytes 258056 | tf_op jit(solution)/shard_map/ppermute | solution.py:199
  64.8 7.3 %collective-permute-start.16 = (bf16[48,896]{1,0:T(8,128)(2,1)S(1)}, bf16[48,896]{1,0:T(8,128)(2,1)S(1)}, u32[]{:S(2)}, u32[]{:S(2)}) collective-permute-start(bf16[48,896]{1,0:T(8,128)(2,1)S(1)} %get-tuple-element.53), channel_id=1, source_target_pairs={{0,4},{1,5},{2,6},{3,7},{4,0},{5,1},{6,2},{7,3},{8,12},{9,13},{10,... | collective-permute-start | bytes 258056 | tf_op jit(solution)/shard_map/ppermute | solution.py:199
  65.9 11.3 %collective-permute-start.17 = (bf16[48,896]{1,0:T(8,128)(2,1)S(1)}, bf16[48,896]{1,0:T(8,128)(2,1)S(1)}, u32[]{:S(2)}, u32[]{:S(2)}) collective-permute-start(bf16[48,896]{1,0:T(8,128)(2,1)S(1)} %get-tuple-element.54), channel_id=1, source_target_pairs={{0,5},{1,4},{2,7},{3,6},{4,1},{5,0},{6,3},{7,2},{8,13},{9,12},{10,... | collective-permute-start | bytes 258056 | tf_op jit(solution)/shard_map/ppermute | solution.py:199
  67.5 13.7 %collective-permute-start.18 = (bf16[48,896]{1,0:T(8,128)(2,1)S(1)}, bf16[48,896]{1,0:T(8,128)(2,1)S(1)}, u32[]{:S(2)}, u32[]{:S(2)}) collective-permute-start(bf16[48,896]{1,0:T(8,128)(2,1)S(1)} %get-tuple-element.55), channel_id=1, source_target_pairs={{0,6},{1,7},{2,4},{3,5},{4,2},{5,3},{6,0},{7,1},{8,14},{9,15},{10,... | collective-permute-start | bytes 258056 | tf_op jit(solution)/shard_map/ppermute | solution.py:199
  69.1 14.0 %collective-permute-start.19 = (bf16[48,896]{1,0:T(8,128)(2,1)S(1)}, bf16[48,896]{1,0:T(8,128)(2,1)S(1)}, u32[]{:S(2)}, u32[]{:S(2)}) collective-permute-start(bf16[48,896]{1,0:T(8,128)(2,1)S(1)} %get-tuple-element.56), channel_id=1, source_target_pairs={{0,7},{1,6},{2,5},{3,4},{4,3},{5,2},{6,1},{7,0},{8,15},{9,14},{10,... | collective-permute-start | bytes 258056 | tf_op jit(solution)/shard_map/ppermute | solution.py:199
